TPU v7x, 512 devices: a whole 4x4x16 slice. The times are simulated.
512 devices in a mesh: ctx: 64 (over x, z), kvh: 8 (over y, core).
Axes of the slice: x: 4, y: 4, z: 16, core: 2. Of those that a mesh axis runs over, the one named last changes fastest.
Arguments:
- queries: bfloat16 [16384, 8192], P(('ctx', 'kvh')), may hold values from -36 to 36
- keys: bfloat16 [16384, 1024], P(('ctx', 'kvh')), may hold values from -4 to 4
- values: bfloat16 [16384, 1024], P(('ctx', 'kvh')), may hold values from -6 to 6
- documents: int32 [16384], replicated, may hold values from 0 to 84, never falling along the last dimension, each value on 1 to 768 neighbouring positions
- grad_out: bfloat16 [16384, 8192], P(('ctx', 'kvh')), may hold values from -6 to 6
Outputs:
- attended: bfloat16 [16384, 8192], P(('ctx', 'kvh'))
- grad_queries: bfloat16 [16384, 8192], P(('ctx', 'kvh'))
- grad_keys: bfloat16 [16384, 1024], P(('ctx', 'kvh'))
- grad_values: bfloat16 [16384, 1024], P(('ctx', 'kvh'))
Inputs may be any that keep to these rules, and one draw needn't show every extreme that they name: `documents`: document numbers never fall along the window; every document has 1 to 768 positions, and one has exactly 768.
All inputs are finite; a program needn't handle non-finite values.
Results may differ from a plain program's by a relative error of at most 0.03.
Values may be sent and summed in bfloat16 or wider, within the bound.
A program may use at most 64 MiB of HBM per device.

v0:
```python
import math

import jax
import jax.numpy as jnp
from jax import lax
from jax.sharding import PartitionSpec as P

HD = 128
REACH = 3


def from_behind(array, axis, by):
    devices = lax.axis_size(axis)
    pairs = [(i, i + by) for i in range(devices) if 0 <= i + by < devices]
    return lax.ppermute(array, axis, pairs)


def body(queries, keys, values, documents, grad_out):
    query_heads, key_heads, value_heads, grad_heads = (
        lax.all_to_all(queries, "kvh", split_axis=1, concat_axis=0, tiled=True),
        lax.all_to_all(keys, "kvh", split_axis=1, concat_axis=0, tiled=True),
        lax.all_to_all(values, "kvh", split_axis=1, concat_axis=0, tiled=True),
        lax.all_to_all(grad_out, "kvh", split_axis=1, concat_axis=0, tiled=True),
    )
    positions = query_heads.shape[0]
    local_kv = key_heads.shape[1] // HD
    group = query_heads.shape[1] // key_heads.shape[1]
    scale = 1.0 / math.sqrt(HD)
    query_four = query_heads.reshape(positions, local_kv, group, HD)
    grad_four = grad_heads.reshape(positions, local_kv, group, HD)
    shard = lax.axis_index("ctx")
    margin = REACH * positions
    width = margin + positions
    query_start = shard * positions
    padded_docs = jnp.concatenate([jnp.full((margin,), -1, jnp.int32), documents])
    query_docs = lax.dynamic_slice_in_dim(padded_docs, query_start + margin, positions, 0)
    key_docs = lax.dynamic_slice_in_dim(padded_docs, query_start, width, 0)
    query_pos = margin + jnp.arange(positions, dtype=jnp.int32)
    key_pos = jnp.arange(width, dtype=jnp.int32)
    visible = (key_docs[None, :] == query_docs[:, None]) & (key_pos[None, :] <= query_pos[:, None])
    earlier = []
    for distance in range(1, REACH + 1):
        earlier.append(from_behind((key_heads, value_heads), "ctx", distance))
    ordered = earlier[::-1]
    key_all = jnp.concatenate([pair[0] for pair in ordered] + [key_heads], 0).reshape(
        width, local_kv, HD
    )
    value_all = jnp.concatenate([pair[1] for pair in ordered] + [value_heads], 0).reshape(
        width, local_kv, HD
    )
    count = max(1, width // 512)
    while width % count:
        count -= 1
    span = width // count
    pieces = []
    for number in range(count):
        seen = visible[:, number * span : (number + 1) * span]
        pieces.append(
            (
                key_all[number * span : (number + 1) * span],
                value_all[number * span : (number + 1) * span],
                seen,
                jnp.any(seen),
            )
        )
    peak = jnp.full((local_kv, group, positions), -1e30, jnp.float32)
    summed = jnp.zeros((local_kv, group, positions), jnp.float32)
    kept_scores = []
    for key_piece, value_piece, seen, needed in pieces:
        gather_peak = peak
        gather_summed = summed
        fresh_scores = (
            jnp.einsum("qhgd,khd->hgqk", query_four, key_piece, preferred_element_type=jnp.float32)
            * scale
        )
        masked = jnp.where(seen, fresh_scores, -1e30)
        fresh = jnp.maximum(gather_peak, jnp.max(masked, axis=-1))
        gather_summed = gather_summed * jnp.exp(gather_peak - fresh) + jnp.sum(
            jnp.where(seen, jnp.exp(masked - fresh[..., None]), 0.0), axis=-1
        )
        peak = fresh
        summed = gather_summed
        piece_scores = fresh_scores
        kept_scores.append(piece_scores)
    log_total = (peak + jnp.log(summed))[..., None]

    def probs_of(piece_scores, seen):
        return jnp.where(seen, jnp.exp(piece_scores - log_total), 0.0)

    output_sum = jnp.zeros((positions, local_kv, group, HD), jnp.float32)
    for (key_piece, value_piece, seen, needed), piece_scores in zip(pieces, kept_scores):
        add_weights = probs_of(piece_scores, seen).astype(jnp.bfloat16)
        output_sum = output_sum + jnp.einsum(
            "hgqk,khd->qhgd", add_weights, value_piece, preferred_element_type=jnp.float32
        )
    attended = output_sum.astype(jnp.bfloat16)
    delta = jnp.sum(grad_four.astype(jnp.float32) * attended.astype(jnp.float32), axis=-1)
    delta = jnp.transpose(delta, (1, 2, 0))[..., None]
    query_grad_sum = jnp.zeros((positions, local_kv, group, HD), jnp.float32)
    blank = jnp.zeros((span, local_kv, HD), jnp.float32)
    key_terms = []
    value_terms = []
    for (key_piece, value_piece, seen, needed), piece_scores in zip(pieces, kept_scores):
        probs = probs_of(piece_scores, seen)
        weights = probs.astype(jnp.bfloat16)
        grad_weights = jnp.einsum(
            "qhgd,khd->hgqk", grad_four, value_piece, preferred_element_type=jnp.float32
        )
        grad_scores = (probs * (grad_weights - delta)).astype(jnp.bfloat16)
        query_term = scale * jnp.einsum(
            "hgqk,khd->qhgd", grad_scores, key_piece, preferred_element_type=jnp.float32
        )
        key_term = scale * jnp.einsum(
            "hgqk,qhgd->khd", grad_scores, query_four, preferred_element_type=jnp.float32
        )
        value_term = jnp.einsum(
            "hgqk,qhgd->khd", weights, grad_four, preferred_element_type=jnp.float32
        )
        query_grad_sum, key_term, value_term = (
            (query_grad_sum, blank, blank)[0] + query_term,
            key_term,
            value_term,
        )
        key_terms.append(key_term)
        value_terms.append(value_term)
    key_parts = jnp.concatenate(key_terms, 0).reshape(REACH + 1, positions, local_kv * HD)
    value_parts = jnp.concatenate(value_terms, 0).reshape(REACH + 1, positions, local_kv * HD)
    own_keys = key_parts[REACH]
    own_values = value_parts[REACH]
    for distance in range(1, REACH + 1):
        got_keys, got_values = from_behind(
            (key_parts[REACH - distance], value_parts[REACH - distance]), "ctx", -distance
        )
        own_keys = own_keys + got_keys
        own_values = own_values + got_values
    attended_rows = attended.reshape(positions, local_kv * group * HD)
    query_grads = query_grad_sum.astype(jnp.bfloat16).reshape(positions, local_kv * group * HD)
    key_grads = own_keys.astype(jnp.bfloat16)
    value_grads = own_values.astype(jnp.bfloat16)
    back = (
        lax.all_to_all(attended_rows, "kvh", split_axis=0, concat_axis=1, tiled=True),
        lax.all_to_all(query_grads, "kvh", split_axis=0, concat_axis=1, tiled=True),
        lax.all_to_all(key_grads, "kvh", split_axis=0, concat_axis=1, tiled=True),
        lax.all_to_all(value_grads, "kvh", split_axis=0, concat_axis=1, tiled=True),
    )
    return (back[0], back[1], back[2], back[3])


def solution(mesh):
    return jax.shard_map(
        body,
        mesh=mesh,
        in_specs=(
            P(("ctx", "kvh"), None),
            P(("ctx", "kvh"), None),
            P(("ctx", "kvh"), None),
            P(),
            P(("ctx", "kvh"), None),
        ),
        out_specs=(
            P(("ctx", "kvh"), None),
            P(("ctx", "kvh"), None),
            P(("ctx", "kvh"), None),
            P(("ctx", "kvh"), None),
        ),
        check_vma=False,
    )
```

profile of v0, /device:TPU:7, one launch (start us, length us, event | category | flops | bytes accessed | tf_op | source)
XLA Modules:
  0.0 165.7 jit_solution(5529614426440652957)
XLA Ops:
  2.1 5.1 %all-to-all-start.1 = ((bf16[32,8,128]{2,0,1:T(8,128)(2,1)}), bf16[32,8,128]{2,0,1:T(8,128)(2,1)S(1)}, u32[]{:S(2)}, u32[]{:S(2)}) async-start(bf16[32,8,128]{2,0,1:T(8,128)(2,1)} %copy_bitcast_fusion.4), calls=%async_computation.1 | async-start | bytes 131072 | tf_op jit(solution)/shard_map/all_to_all | solution.py:21
  8.7 3.4 %all-to-all-done.1 = bf16[32,8,128]{2,0,1:T(8,128)(2,1)S(1)} async-done(((bf16[32,8,128]{2,0,1:T(8,128)(2,1)}), bf16[32,8,128]{2,0,1:T(8,128)(2,1)S(1)}, u32[]{:S(2)}, u32[]{:S(2)}) %all-to-all-start.1) | async-done | bytes 65568 | tf_op jit(solution)/shard_map/all_to_all | solution.py:21
  12.1 4.0 %all-to-all-start = ((bf16[32,8,128]{2,0,1:T(8,128)(2,1)}), bf16[32,8,128]{2,0,1:T(8,128)(2,1)S(1)}, u32[]{:S(2)}, u32[]{:S(2)}) async-start(bf16[32,8,128]{2,0,1:T(8,128)(2,1)} %copy_bitcast_fusion.5), calls=%async_computation | async-start | bytes 131072 | tf_op jit(solution)/shard_map/all_to_all | solution.py:22
  18.0 3.0 %all-to-all-done = bf16[32,8,128]{2,0,1:T(8,128)(2,1)S(1)} async-done(((bf16[32,8,128]{2,0,1:T(8,128)(2,1)}), bf16[32,8,128]{2,0,1:T(8,128)(2,1)S(1)}, u32[]{:S(2)}, u32[]{:S(2)}) %all-to-all-start) | async-done | bytes 65568 | tf_op jit(solution)/shard_map/all_to_all | solution.py:22
  21.0 4.2 %all-to-all-start.2 = ((bf16[32,8,1024]{2,0,1:T(8,128)(2,1)}), bf16[32,8,1024]{2,0,1:T(8,128)(2,1)S(1)}, u32[]{:S(2)}, u32[]{:S(2)}) async-start(bf16[32,8,1024]{2,0,1:T(8,128)(2,1)} %bitcast.276), calls=%async_computation.2 | async-start | bytes 1048576 | tf_op jit(solution)/shard_map/all_to_all | solution.py:20
  28.9 3.5 %collective-permute-start.4 = (bf16[256,128]{1,0:T(8,128)(2,1)S(1)}, bf16[256,128]{1,0:T(8,128)(2,1)S(1)}, u32[]{:S(2)}, u32[]{:S(2)}) collective-permute-start(bf16[256,128]{1,0:T(8,128)(2,1)S(1)} %bitcast.287), channel_id=1, source_target_pairs={{0,8},{8,16},{16,24},{24,32},{32,40},{40,48},{48,56},{56,64},{64,7... | collective-permute-start | bytes 196616 | tf_op jit(solution)/shard_map/ppermute | solution.py:15
  32.4 2.1 %all-to-all-done.2 = bf16[32,8,1024]{2,0,1:T(8,128)(2,1)S(1)} async-done(((bf16[32,8,1024]{2,0,1:T(8,128)(2,1)}), bf16[32,8,1024]{2,0,1:T(8,128)(2,1)S(1)}, u32[]{:S(2)}, u32[]{:S(2)}) %all-to-all-start.2) | async-done | bytes 524320 | tf_op jit(solution)/shard_map/all_to_all | solution.py:20
  34.6 4.4 %all-to-all-start.4 = ((bf16[32,8,1024]{2,0,1:T(8,128)(2,1)}), bf16[32,8,1024]{2,0,1:T(8,128)(2,1)S(1)}, u32[]{:S(2)}, u32[]{:S(2)}) async-start(bf16[32,8,1024]{2,0,1:T(8,128)(2,1)} %bitcast.275), calls=%async_computation.4 | async-start | bytes 1048576 | tf_op jit(solution)/shard_map/all_to_all | solution.py:23
  39.7 3.5 %collective-permute-start.5 = (bf16[256,128]{0,1:T(8,128)(2,1)}, bf16[256,128]{0,1:T(8,128)(2,1)S(1)}, u32[]{:S(2)}, u32[]{:S(2)}) collective-permute-start(bf16[256,128]{0,1:T(8,128)(2,1)} %copy.84), channel_id=1, source_target_pairs={{0,8},{8,16},{16,24},{24,32},{32,40},{40,48},{48,56},{56,64},{64,7... | collective-permute-start | bytes 196616 | tf_op jit(solution)/shard_map/ppermute | solution.py:15
  43.2 4.9 %collective-permute-start.1 = (bf16[256,128]{0,1:T(8,128)(2,1)}, bf16[256,128]{0,1:T(8,128)(2,1)}, u32[]{:S(2)}, u32[]{:S(2)}) collective-permute-start(bf16[256,128]{0,1:T(8,128)(2,1)} %copy.84), channel_id=1, source_target_pairs={{0,16},{8,24},{16,32},{24,40},{32,48},{40,56},{48,64},{56,72},{64,... | collective-permute-start | bytes 196616 | tf_op jit(solution)/shard_map/ppermute | solution.py:15
  48.1 7.5 %collective-permute-start = (bf16[256,128]{0,1:T(8,128)(2,1)}, bf16[256,128]{0,1:T(8,128)(2,1)}, u32[]{:S(2)}, u32[]{:S(2)}) collective-permute-start(bf16[256,128]{0,1:T(8,128)(2,1)} %copy.84), channel_id=1, source_target_pairs={{0,24},{8,32},{16,40},{24,48},{32,56},{40,64},{48,72},{56,80},{64,... | collective-permute-start | bytes 196616 | tf_op jit(solution)/shard_map/ppermute | solution.py:15
  55.6 6.1 %collective-permute-start.3 = (bf16[256,128]{1,0:T(8,128)(2,1)S(1)}, bf16[256,128]{1,0:T(8,128)(2,1)S(1)}, u32[]{:S(2)}, u32[]{:S(2)}) collective-permute-start(bf16[256,128]{1,0:T(8,128)(2,1)S(1)} %bitcast.288), channel_id=1, source_target_pairs={{0,16},{8,24},{16,32},{24,40},{32,48},{40,56},{48,64},{56,72},{64,... | collective-permute-start | bytes 196616 | tf_op jit(solution)/shard_map/ppermute | solution.py:15
  61.9 3.6 %collective-permute-start.2 = (bf16[256,128]{1,0:T(8,128)(2,1)S(1)}, bf16[256,128]{1,0:T(8,128)(2,1)S(1)}, u32[]{:S(2)}, u32[]{:S(2)}) collective-permute-start(bf16[256,128]{1,0:T(8,128)(2,1)S(1)} %bitcast.289), channel_id=1, source_target_pairs={{0,24},{8,32},{16,40},{24,48},{32,56},{40,64},{48,72},{56,80},{64,... | collective-permute-start | bytes 196616 | tf_op jit(solution)/shard_map/ppermute | solution.py:15
  65.4 2.8 %fusion.9 = (f32[8,256]{1,0:T(8,128)S(1)}, f32[512,256,8]{1,0,2:T(8,128)}) fusion(pred[256,512]{0,1:T(8,128)(4,1)S(1)} %get-tuple-element.9, bf16[256,8,128]{2,1,0:T(8,128)(2,1)S(1)} %bitcast.277, bf16[256,128]{1,0:T(8,128)(2,1)S(1)} %bitcast.290, bf16[256,128]{1,0:T(8,128)(2,1)S(1)} %collective-permute-done.4), kind=kOutput, calls=%fused_computation.17 | convolution fusion | flops 271841280 | bytes 4988928 | tf_op jit(solution)/shard_map/qhgd,khd->hgqk/dot_general | solution.py:73
  68.3 4.7 %collective-permute-done.2 = bf16[256,128]{1,0:T(8,128)(2,1)S(1)} collective-permute-done((bf16[256,128]{1,0:T(8,128)(2,1)S(1)}, bf16[256,128]{1,0:T(8,128)(2,1)S(1)}, u32[]{:S(2)}, u32[]{:S(2)}) %collective-permute-start.2) | collective-permute-done | bytes 65568 | tf_op jit(solution)/shard_map/ppermute | solution.py:15
  82.5 2.7 %collective-permute-start.10 = (f32[256,128]{1,0:T(8,128)}, f32[256,128]{1,0:T(8,128)}, u32[]{:S(2)}, u32[]{:S(2)}) collective-permute-start(f32[256,128]{1,0:T(8,128)} %get-tuple-element.4), channel_id=1, source_target_pairs={{16,0},{24,8},{32,16},{40,24},{48,32},{56,40},{64,48},{72,56},{80,... | collective-permute-start | bytes 393224 | tf_op jit(solution)/shard_map/ppermute | solution.py:15
  85.3 4.3 %collective-permute-start.11 = (f32[256,128]{1,0:T(8,128)}, f32[256,128]{1,0:T(8,128)}, u32[]{:S(2)}, u32[]{:S(2)}) collective-permute-start(f32[256,128]{1,0:T(8,128)} %get-tuple-element.5), channel_id=1, source_target_pairs={{24,0},{32,8},{40,16},{48,24},{56,32},{64,40},{72,48},{80,56},{88,... | collective-permute-start | bytes 393224 | tf_op jit(solution)/shard_map/ppermute | solution.py:15
  89.6 2.8 %fusion.73 = f32[128,8,256]{2,0,1:T(8,128)} fusion(bf16[256,128]{0,1:T(8,128)(2,1)} %copy.84, bf16[256,128]{0,1:T(8,128)(2,1)S(1)} %collective-permute-done.5, f32[512,256,8]{1,0,2:T(8,128)S(1)} %copy-done.3, f32[8,256]{1,0:T(8,128)S(1)} %log_add_fusion, pred[256,512]{0,1:T(8,128)(4,1)S(1)} %get-tuple-element.9), kind=kOutput, calls=%fused_computation.81 | convolution fusion | flops 272891904 | bytes 5513216 | tf_op jit(solution)/shard_map/hgqk,khd->qhgd/dot_general | solution.py:93
  93.2 3.8 %multiply_reduce_fusion = (f32[256,8]{0,1:T(8,128)S(1)}, bf16[256,1,8,128]{0,3,2,1:T(8,128)(2,1)S(1)}) fusion(f32[256,1,8,128]{0,3,2,1:T(8,128)S(1)} %copy.99, f32[128,8,256]{2,0,1:T(8,128)} %fusion.73, f32[512,256,8]{1,0,2:T(8,128)} %copy-done.1, f32[8,256]{1,0:T(8,128)S(1)} %log_add_fusion, pred[256,512]{0,1:T(8,128)(4,1)S(1)} %get-tuple-element.8, ...), kind=kOutput, calls=%fused_computation.45 | convolution fusion | flops 274200576 | bytes 7094272 | tf_op jit(solution)/shard_map/hgqk,khd->qhgd/dot_general | solution.py:93
  97.1 2.4 %fusion.1 = bf16[1,8,256,512]{2,3,1,0:T(8,128)(2,1)S(1)} fusion(f32[512,256,8]{1,0,2:T(8,128)S(1)} %copy-done.4, f32[8,256]{1,0:T(8,128)S(1)} %bitcast.301, f32[8,256]{1,0:T(8,128)S(1)} %log_add_fusion, pred[256,512]{0,1:T(8,128)(4,1)S(1)} %get-tuple-element.9, bf16[256,8,128]{2,1,0:T(8,128)(2,1)S(1)} %bitcast.296, bf16[256,128]{0,1:T(8,128)(2,1)} %copy.84, ...), kind=kOutput, calls=%fused_computation.2 | convolution fusion | flops 274989056 | bytes 7094272 | tf_op jit(solution)/shard_map/qhgd,khd->hgqk/dot_general | solution.py:106
  100.3 2.3 %fusion.3 = bf16[1,8,256,512]{2,3,1,0:T(8,128)(2,1)S(1)} fusion(f32[512,256,8]{1,0,2:T(8,128)S(1)} %copy-done.2, f32[8,256]{1,0:T(8,128)S(1)} %bitcast.302, f32[8,256]{1,0:T(8,128)S(1)} %log_add_fusion, pred[256,512]{0,1:T(8,128)(4,1)S(1)} %get-tuple-element.8, bf16[256,8,128]{2,1,0:T(8,128)(2,1)S(1)} %bitcast.297, ...), kind=kOutput, calls=%fused_computation.5 | convolution fusion | flops 274989056 | bytes 7094272 | tf_op jit(solution)/shard_map/qhgd,khd->hgqk/dot_general | solution.py:106
  103.4 2.9 %collective-permute-start.6 = (f32[256,128]{1,0:T(8,128)S(1)}, f32[256,128]{1,0:T(8,128)S(1)}, u32[]{:S(2)}, u32[]{:S(2)}) collective-permute-start(f32[256,128]{1,0:T(8,128)S(1)} %slice_bitcast_fusion.6), channel_id=1, source_target_pairs={{8,0},{16,8},{24,16},{32,24},{40,32},{48,40},{56,48},{64,56},{72,6... | collective-permute-start | bytes 393224 | tf_op jit(solution)/shard_map/ppermute | solution.py:15
  106.3 2.1 %collective-permute-start.7 = (f32[256,128]{1,0:T(8,128)S(1)}, f32[256,128]{1,0:T(8,128)S(1)}, u32[]{:S(2)}, u32[]{:S(2)}) collective-permute-start(f32[256,128]{1,0:T(8,128)S(1)} %get-tuple-element.6), channel_id=1, source_target_pairs={{16,0},{24,8},{32,16},{40,24},{48,32},{56,40},{64,48},{72,56},{80,... | collective-permute-start | bytes 393224 | tf_op jit(solution)/shard_map/ppermute | solution.py:15
  108.9 5.5 %collective-permute-start.8 = (f32[256,128]{1,0:T(8,128)S(1)}, f32[256,128]{1,0:T(8,128)S(1)}, u32[]{:S(2)}, u32[]{:S(2)}) collective-permute-start(f32[256,128]{1,0:T(8,128)S(1)} %get-tuple-element.7), channel_id=1, source_target_pairs={{24,0},{32,8},{40,16},{48,24},{56,32},{64,40},{72,48},{80,56},{88,... | collective-permute-start | bytes 393224 | tf_op jit(solution)/shard_map/ppermute | solution.py:15
  116.2 7.4 %all-to-all-start.7 = ((bf16[8,32,128]{2,1,0:T(8,128)(2,1)}), bf16[8,32,128]{2,1,0:T(8,128)(2,1)S(1)}, u32[]{:S(2)}, u32[]{:S(2)}) async-start(bf16[8,32,128]{2,1,0:T(8,128)(2,1)} %bitcast.76), calls=%async_computation.7 | async-start | bytes 131072 | tf_op jit(solution)/shard_map/all_to_all | solution.py:144
  124.2 4.2 %all-to-all-done.7 = bf16[8,32,128]{2,1,0:T(8,128)(2,1)S(1)} async-done(((bf16[8,32,128]{2,1,0:T(8,128)(2,1)}), bf16[8,32,128]{2,1,0:T(8,128)(2,1)S(1)}, u32[]{:S(2)}, u32[]{:S(2)}) %all-to-all-start.7) | async-done | bytes 65568 | tf_op jit(solution)/shard_map/all_to_all | solution.py:144
  128.4 4.3 %all-to-all-start.6 = ((bf16[8,32,128]{2,1,0:T(8,128)(2,1)}), bf16[8,32,128]{2,1,0:T(8,128)(2,1)S(1)}, u32[]{:S(2)}, u32[]{:S(2)}) async-start(bf16[8,32,128]{2,1,0:T(8,128)(2,1)} %bitcast.56), calls=%async_computation.6 | async-start | bytes 131072 | tf_op jit(solution)/shard_map/all_to_all | solution.py:143
  132.7 2.1 %fusion.32 = bf16[256,1,8,128]{0,3,2,1:T(8,128)(2,1)S(1)} fusion(f32[128,8,256]{2,0,1:T(8,128)S(1)} %fusion.16, bf16[1,8,256,512]{2,3,1,0:T(8,128)(2,1)} %copy-done.5, bf16[256,128]{1,0:T(8,128)(2,1)S(1)} %copy-done.11, bf16[256,128]{1,0:T(8,128)(2,1)S(1)} %copy-done.13), kind=kOutput, calls=%fused_computation.35 | convolution fusion | flops 269484032 | bytes 3801088 | tf_op jit(solution)/shard_map/hgqk,khd->qhgd/dot_general | solution.py:110
  137.6 4.2 %all-to-all-start.5 = ((bf16[8,32,1024]{2,1,0:T(8,128)(2,1)}), bf16[8,32,1024]{2,1,0:T(8,128)(2,1)S(1)}, u32[]{:S(2)}, u32[]{:S(2)}) async-start(bf16[8,32,1024]{2,1,0:T(8,128)(2,1)} %all_to_all.126), calls=%async_computation.5 | async-start | bytes 1048576 | tf_op jit(solution)/shard_map/all_to_all | solution.py:142
  143.1 8.0 %all-to-all-done.5 = bf16[8,32,1024]{2,1,0:T(8,128)(2,1)S(1)} async-done(((bf16[8,32,1024]{2,1,0:T(8,128)(2,1)}), bf16[8,32,1024]{2,1,0:T(8,128)(2,1)S(1)}, u32[]{:S(2)}, u32[]{:S(2)}) %all-to-all-start.5) | async-done | bytes 524320 | tf_op jit(solution)/shard_map/all_to_all | solution.py:142
  151.1 4.4 %all-to-all-start.3 = ((bf16[8,32,1024]{2,1,0:T(8,128)(2,1)}), bf16[8,32,1024]{2,1,0:T(8,128)(2,1)S(1)}, u32[]{:S(2)}, u32[]{:S(2)}) async-start(bf16[8,32,1024]{2,1,0:T(8,128)(2,1)} %all_to_all.119), calls=%async_computation.3 | async-start | bytes 1048576 | tf_op jit(solution)/shard_map/all_to_all | solution.py:141
  157.6 7.3 %all-to-all-done.3 = bf16[8,32,1024]{2,1,0:T(8,128)(2,1)S(1)} async-done(((bf16[8,32,1024]{2,1,0:T(8,128)(2,1)}), bf16[8,32,1024]{2,1,0:T(8,128)(2,1)S(1)}, u32[]{:S(2)}, u32[]{:S(2)}) %all-to-all-start.3) | async-done | bytes 524320 | tf_op jit(solution)/shard_map/all_to_all | solution.py:141
  (88 shorter events, 31.0 us)
Async XLA Ops:
  2.1 10.0 %all-to-all-start.1 = ((bf16[32,8,128]{2,0,1:T(8,128)(2,1)}), bf16[32,8,128]{2,0,1:T(8,128)(2,1)S(1)}, u32[]{:S(2)}, u32[]{:S(2)}) async-start(bf16[32,8,128]{2,0,1:T(8,128)(2,1)} %copy_bitcast_fusion.4), calls=%async_computation.1 | async-start | bytes 131072 | tf_op jit(solution)/shard_map/all_to_all | solution.py:21
  12.1 8.9 %all-to-all-start = ((bf16[32,8,128]{2,0,1:T(8,128)(2,1)}), bf16[32,8,128]{2,0,1:T(8,128)(2,1)S(1)}, u32[]{:S(2)}, u32[]{:S(2)}) async-start(bf16[32,8,128]{2,0,1:T(8,128)(2,1)} %copy_bitcast_fusion.5), calls=%async_computation | async-start | bytes 131072 | tf_op jit(solution)/shard_map/all_to_all | solution.py:22
  21.0 13.6 %all-to-all-start.2 = ((bf16[32,8,1024]{2,0,1:T(8,128)(2,1)}), bf16[32,8,1024]{2,0,1:T(8,128)(2,1)S(1)}, u32[]{:S(2)}, u32[]{:S(2)}) async-start(bf16[32,8,1024]{2,0,1:T(8,128)(2,1)} %bitcast.276), calls=%async_computation.2 | async-start | bytes 1048576 | tf_op jit(solution)/shard_map/all_to_all | solution.py:20
  28.9 33.0 %collective-permute-start.4 = (bf16[256,128]{1,0:T(8,128)(2,1)S(1)}, bf16[256,128]{1,0:T(8,128)(2,1)S(1)}, u32[]{:S(2)}, u32[]{:S(2)}) collective-permute-start(bf16[256,128]{1,0:T(8,128)(2,1)S(1)} %bitcast.287), channel_id=1, source_target_pairs={{0,8},{8,16},{16,24},{24,32},{32,40},{40,48},{48,56},{56,64},{64,7... | collective-permute-start | bytes 196616 | tf_op jit(solution)/shard_map/ppermute | solution.py:15
  34.6 33.6 %all-to-all-start.4 = ((bf16[32,8,1024]{2,0,1:T(8,128)(2,1)}), bf16[32,8,1024]{2,0,1:T(8,128)(2,1)S(1)}, u32[]{:S(2)}, u32[]{:S(2)}) async-start(bf16[32,8,1024]{2,0,1:T(8,128)(2,1)} %bitcast.275), calls=%async_computation.4 | async-start | bytes 1048576 | tf_op jit(solution)/shard_map/all_to_all | solution.py:23
  39.7 45.6 %collective-permute-start.5 = (bf16[256,128]{0,1:T(8,128)(2,1)}, bf16[256,128]{0,1:T(8,128)(2,1)S(1)}, u32[]{:S(2)}, u32[]{:S(2)}) collective-permute-start(bf16[256,128]{0,1:T(8,128)(2,1)} %copy.84), channel_id=1, source_target_pairs={{0,8},{8,16},{16,24},{24,32},{32,40},{40,48},{48,56},{56,64},{64,7... | collective-permute-start | bytes 196616 | tf_op jit(solution)/shard_map/ppermute | solution.py:15
  43.2 50.0 %collective-permute-start.1 = (bf16[256,128]{0,1:T(8,128)(2,1)}, bf16[256,128]{0,1:T(8,128)(2,1)}, u32[]{:S(2)}, u32[]{:S(2)}) collective-permute-start(bf16[256,128]{0,1:T(8,128)(2,1)} %copy.84), channel_id=1, source_target_pairs={{0,16},{8,24},{16,32},{24,40},{32,48},{40,56},{48,64},{56,72},{64,... | collective-permute-start | bytes 196616 | tf_op jit(solution)/shard_map/ppermute | solution.py:15
  48.1 45.1 %collective-permute-start = (bf16[256,128]{0,1:T(8,128)(2,1)}, bf16[256,128]{0,1:T(8,128)(2,1)}, u32[]{:S(2)}, u32[]{:S(2)}) collective-permute-start(bf16[256,128]{0,1:T(8,128)(2,1)} %copy.84), channel_id=1, source_target_pairs={{0,24},{8,32},{16,40},{24,48},{32,56},{40,64},{48,72},{56,80},{64,... | collective-permute-start | bytes 196616 | tf_op jit(solution)/shard_map/ppermute | solution.py:15
  55.6 12.7 %collective-permute-start.3 = (bf16[256,128]{1,0:T(8,128)(2,1)S(1)}, bf16[256,128]{1,0:T(8,128)(2,1)S(1)}, u32[]{:S(2)}, u32[]{:S(2)}) collective-permute-start(bf16[256,128]{1,0:T(8,128)(2,1)S(1)} %bitcast.288), channel_id=1, source_target_pairs={{0,16},{8,24},{16,32},{24,40},{32,48},{40,56},{48,64},{56,72},{64,... | collective-permute-start | bytes 196616 | tf_op jit(solution)/shard_map/ppermute | solution.py:15
  61.8 12.0 %copy-start.8 = (bf16[256,128]{1,0:T(8,128)(2,1)}, bf16[256,128]{1,0:T(8,128)(2,1)S(1)}, u32[]{:S(2)}) copy-start(bf16[256,128]{1,0:T(8,128)(2,1)S(1)} %collective-permute-done.4) | copy-start | bytes 196612
  61.9 11.2 %collective-permute-start.2 = (bf16[256,128]{1,0:T(8,128)(2,1)S(1)}, bf16[256,128]{1,0:T(8,128)(2,1)S(1)}, u32[]{:S(2)}, u32[]{:S(2)}) collective-permute-start(bf16[256,128]{1,0:T(8,128)(2,1)S(1)} %bitcast.289), channel_id=1, source_target_pairs={{0,24},{8,32},{16,40},{24,48},{32,56},{40,64},{48,72},{56,80},{64,... | collective-permute-start | bytes 196616 | tf_op jit(solution)/shard_map/ppermute | solution.py:15
  68.3 10.0 %copy-start.6 = (bf16[32,8,8,128]{3,2,1,0:T(8,128)(2,1)}, bf16[32,8,8,128]{3,2,1,0:T(8,128)(2,1)S(1)}, u32[]{:S(2)}) copy-start(bf16[32,8,8,128]{3,2,1,0:T(8,128)(2,1)S(1)} %copy.135) | copy-start | bytes 1572868
  68.3 6.6 %copy-start.10 = (bf16[256,128]{1,0:T(8,128)(2,1)}, bf16[256,128]{1,0:T(8,128)(2,1)S(1)}, u32[]{:S(2)}) copy-start(bf16[256,128]{1,0:T(8,128)(2,1)S(1)} %collective-permute-done.3) | copy-start | bytes 196612
  73.8 4.5 %copy-start.1 = (f32[512,256,8]{1,0,2:T(8,128)}, f32[512,256,8]{1,0,2:T(8,128)S(1)}, u32[]{:S(2)}) copy-start(f32[512,256,8]{1,0,2:T(8,128)S(1)} %get-tuple-element.13) | copy-start | bytes 12582916
  78.3 14.1 %copy-start.14 = (f32[512,1,128]{2,0,1:T(8,128)}, f32[512,1,128]{2,0,1:T(8,128)S(1)}, u32[]{:S(2)}) copy-start(f32[512,1,128]{2,0,1:T(8,128)S(1)} %convolution_bitcast_fusion.1) | copy-start | bytes 786436
  79.9 29.0 %collective-permute-start.9 = (f32[256,128]{1,0:T(8,128)}, f32[256,128]{1,0:T(8,128)}, u32[]{:S(2)}, u32[]{:S(2)}) collective-permute-start(f32[256,128]{1,0:T(8,128)} %slice_bitcast_fusion.2), channel_id=1, source_target_pairs={{8,0},{16,8},{24,16},{32,24},{40,32},{48,40},{56,48},{64,56},{72,6... | collective-permute-start | bytes 393224 | tf_op jit(solution)/shard_map/ppermute | solution.py:15
  82.5 31.9 %collective-permute-start.10 = (f32[256,128]{1,0:T(8,128)}, f32[256,128]{1,0:T(8,128)}, u32[]{:S(2)}, u32[]{:S(2)}) collective-permute-start(f32[256,128]{1,0:T(8,128)} %get-tuple-element.4), channel_id=1, source_target_pairs={{16,0},{24,8},{32,16},{40,24},{48,32},{56,40},{64,48},{72,56},{80,... | collective-permute-start | bytes 393224 | tf_op jit(solution)/shard_map/ppermute | solution.py:15
  85.3 7.3 %copy-start.16 = (bf16[256,128]{0,1:T(8,128)(2,1)}, bf16[256,128]{0,1:T(8,128)(2,1)S(1)}, u32[]{:S(2)}) copy-start(bf16[256,128]{0,1:T(8,128)(2,1)S(1)} %collective-permute-done.5) | copy-start | bytes 196612
  85.3 29.2 %collective-permute-start.11 = (f32[256,128]{1,0:T(8,128)}, f32[256,128]{1,0:T(8,128)}, u32[]{:S(2)}, u32[]{:S(2)}) collective-permute-start(f32[256,128]{1,0:T(8,128)} %get-tuple-element.5), channel_id=1, source_target_pairs={{24,0},{32,8},{40,16},{48,24},{56,32},{64,40},{72,48},{80,56},{88,... | collective-permute-start | bytes 393224 | tf_op jit(solution)/shard_map/ppermute | solution.py:15
  93.2 3.9 %copy-start.7 = (bf16[32,8,8,128]{3,2,1,0:T(8,128)(2,1)S(1)}, bf16[32,8,8,128]{3,2,1,0:T(8,128)(2,1)}, u32[]{:S(2)}) copy-start(bf16[32,8,8,128]{3,2,1,0:T(8,128)(2,1)} %copy-done.6) | copy-start | bytes 1572868
  93.2 3.9 %copy-start.17 = (bf16[256,128]{0,1:T(8,128)(2,1)S(1)}, bf16[256,128]{0,1:T(8,128)(2,1)}, u32[]{:S(2)}) copy-start(bf16[256,128]{0,1:T(8,128)(2,1)} %copy-done.16) | copy-start | bytes 196612
  100.3 8.2 %copy-start.9 = (bf16[256,128]{1,0:T(8,128)(2,1)S(1)}, bf16[256,128]{1,0:T(8,128)(2,1)}, u32[]{:S(2)}) copy-start(bf16[256,128]{1,0:T(8,128)(2,1)} %copy-done.8) | copy-start | bytes 196612
  102.6 11.9 %copy-start.15 = (f32[512,1,128]{2,0,1:T(8,128)S(1)}, f32[512,1,128]{2,0,1:T(8,128)}, u32[]{:S(2)}) copy-start(f32[512,1,128]{2,0,1:T(8,128)} %copy-done.14) | copy-start | bytes 786436
  102.6 30.1 %copy-start.11 = (bf16[256,128]{1,0:T(8,128)(2,1)S(1)}, bf16[256,128]{1,0:T(8,128)(2,1)}, u32[]{:S(2)}) copy-start(bf16[256,128]{1,0:T(8,128)(2,1)} %copy-done.10) | copy-start | bytes 196612
  102.6 30.1 %copy-start.13 = (bf16[256,128]{1,0:T(8,128)(2,1)S(1)}, bf16[256,128]{1,0:T(8,128)(2,1)}, u32[]{:S(2)}) copy-start(bf16[256,128]{1,0:T(8,128)(2,1)} %copy-done.12) | copy-start | bytes 196612
  103.4 20.1 %collective-permute-start.6 = (f32[256,128]{1,0:T(8,128)S(1)}, f32[256,128]{1,0:T(8,128)S(1)}, u32[]{:S(2)}, u32[]{:S(2)}) collective-permute-start(f32[256,128]{1,0:T(8,128)S(1)} %slice_bitcast_fusion.6), channel_id=1, source_target_pairs={{8,0},{16,8},{24,16},{32,24},{40,32},{48,40},{56,48},{64,56},{72,6... | collective-permute-start | bytes 393224 | tf_op jit(solution)/shard_map/ppermute | solution.py:15
  106.3 17.3 %collective-permute-start.7 = (f32[256,128]{1,0:T(8,128)S(1)}, f32[256,128]{1,0:T(8,128)S(1)}, u32[]{:S(2)}, u32[]{:S(2)}) collective-permute-start(f32[256,128]{1,0:T(8,128)S(1)} %get-tuple-element.6), channel_id=1, source_target_pairs={{16,0},{24,8},{32,16},{40,24},{48,32},{56,40},{64,48},{72,56},{80,... | collective-permute-start | bytes 393224 | tf_op jit(solution)/shard_map/ppermute | solution.py:15
  108.9 14.6 %collective-permute-start.8 = (f32[256,128]{1,0:T(8,128)S(1)}, f32[256,128]{1,0:T(8,128)S(1)}, u32[]{:S(2)}, u32[]{:S(2)}) collective-permute-start(f32[256,128]{1,0:T(8,128)S(1)} %get-tuple-element.7), channel_id=1, source_target_pairs={{24,0},{32,8},{40,16},{48,24},{56,32},{64,40},{72,48},{80,56},{88,... | collective-permute-start | bytes 393224 | tf_op jit(solution)/shard_map/ppermute | solution.py:15
  116.2 12.2 %all-to-all-start.7 = ((bf16[8,32,128]{2,1,0:T(8,128)(2,1)}), bf16[8,32,128]{2,1,0:T(8,128)(2,1)S(1)}, u32[]{:S(2)}, u32[]{:S(2)}) async-start(bf16[8,32,128]{2,1,0:T(8,128)(2,1)} %bitcast.76), calls=%async_computation.7 | async-start | bytes 131072 | tf_op jit(solution)/shard_map/all_to_all | solution.py:144
  128.4 9.2 %all-to-all-start.6 = ((bf16[8,32,128]{2,1,0:T(8,128)(2,1)}), bf16[8,32,128]{2,1,0:T(8,128)(2,1)S(1)}, u32[]{:S(2)}, u32[]{:S(2)}) async-start(bf16[8,32,128]{2,1,0:T(8,128)(2,1)} %bitcast.56), calls=%async_computation.6 | async-start | bytes 131072 | tf_op jit(solution)/shard_map/all_to_all | solution.py:143
  137.6 13.6 %all-to-all-start.5 = ((bf16[8,32,1024]{2,1,0:T(8,128)(2,1)}), bf16[8,32,1024]{2,1,0:T(8,128)(2,1)S(1)}, u32[]{:S(2)}, u32[]{:S(2)}) async-start(bf16[8,32,1024]{2,1,0:T(8,128)(2,1)} %all_to_all.126), calls=%async_computation.5 | async-start | bytes 1048576 | tf_op jit(solution)/shard_map/all_to_all | solution.py:142
  151.1 13.7 %all-to-all-start.3 = ((bf16[8,32,1024]{2,1,0:T(8,128)(2,1)}), bf16[8,32,1024]{2,1,0:T(8,128)(2,1)S(1)}, u32[]{:S(2)}, u32[]{:S(2)}) async-start(bf16[8,32,1024]{2,1,0:T(8,128)(2,1)} %all_to_all.119), calls=%async_computation.3 | async-start | bytes 1048576 | tf_op jit(solution)/shard_map/all_to_all | solution.py:141
  (6 other events, 16.7 us)
where the time goes:
time: 168 us; the launch traced here: 166 us
  starting transfers between devices  86.5 us (51%)
  waiting for transfers between devices  34.2 us (20%)
  matrix products  20.6 us (12%)
  local copies, waits for them, and re-layouts  17.7 us (11%)
  other arithmetic  5.52 us (3%)
    ppermute x12, starting transfers between devices, from_behind(): return lax.ppermute(array, axis, pairs)  48.6 us
    all_to_all x1, waiting for transfers between devices, body(): lax.all_to_all(query_grads, 'kvh', split_axis=0, concat_axis=1, tiled=True)  8.04 us
    all_to_all x1, starting transfers between devices, body(): lax.all_to_all(value_grads, 'kvh', split_axis=0, concat_axis=1, tiled=True)  7.36 us
    all_to_all x1, waiting for transfers between devices, body(): lax.all_to_all(attended_rows, 'kvh', split_axis=0, concat_axis=1, tiled=T...  7.28 us
    dot_general x2, matrix products, body(): jnp.einsum('hgqk,khd->qhgd', add_weights, value_piece, preferred_element_...  6.59 us
    all_to_all x1, starting transfers between devices, body(): lax.all_to_all(keys, 'kvh', split_axis=1, concat_axis=0, tiled=True)  5.14 us
    dot_general x2, matrix products, body(): jnp.einsum('qhgd,khd->hgqk', grad_four, value_piece, preferred_element_ty...  4.74 us
    ppermute x12, waiting for transfers between devices, from_behind(): return lax.ppermute(array, axis, pairs)  4.73 us
  transfers between devices with their start and end apart: 20, of which 8 were waited for; matrix products, arithmetic and copies ran while one was open for 23% of the time, Pallas kernels for 0%

commit v1 on v0

v1 whole, which is shorter than its diff:
```python
import math

import jax
import jax.numpy as jnp
from jax import lax
from jax.experimental import pallas as pl
from jax.experimental.pallas import tpu as pltpu
from jax.sharding import PartitionSpec as P

HD = 128
REACH = 3
PEERS = 8
ROWS = 32
SHARD = 256
WIN = 1024
SPAN = 896
GW = 1024
SCALE = 1.0 / math.sqrt(HD)
LOG2E = 1.4426950408889634
MESH = pl.DeviceIdType.MESH
F32 = jnp.float32
BF16 = jnp.bfloat16
NT = (((1,), (1,)), ((), ()))
NN = (((1,), (0,)), ((), ()))


def dot(a, b, dims=NN):
    return lax.dot_general(a, b, dims, preferred_element_type=F32)


def kernel(
    q_ref, k_ref, v_ref, doc_ref, go_ref,
    att_ref, gq_ref, gk_ref, gv_ref,
    qb, gb, kw, vw, kt, vt, qall, got, kd, bias, scr, eall, dsall, ob, gqb,
    part, sendk, recvk, fin,
    q_s, q_r, kv_s, kv_r, z_s, z_r, o_s, o_r, g_s, g_r, w_s, w_r, f_s, f_r,
):
    c = lax.axis_index("ctx")
    h = lax.axis_index("kvh")
    shards = lax.axis_size("ctx")
    y = h // 2
    core = h % 2
    after = lax.rem(c + 1, shards)
    before = lax.rem(c + shards - 1, shards)

    def to(i):
        return lax.rem(y + i // 2, 4) * 2 + lax.rem(core + i % 2, 2)

    def source(i):
        return lax.rem(y - i // 2 + 4, 4) * 2 + lax.rem(core - i % 2 + 2, 2)

    def rows_of(p):
        return pl.ds(pl.multiple_of(p * ROWS, ROWS), ROWS)

    def wide(p):
        return pl.ds(pl.multiple_of(p * GW, GW), GW)

    def narrow(p):
        return pl.ds(pl.multiple_of(p * HD, HD), HD)

    own = [
        pltpu.make_async_copy(k_ref.at[:, narrow(h)], kw.at[pl.ds(pl.multiple_of(3 * SHARD + h * ROWS, ROWS), ROWS)], kv_r.at[0, 0]),
        pltpu.make_async_copy(v_ref.at[:, narrow(h)], vw.at[pl.ds(pl.multiple_of(3 * SHARD + h * ROWS, ROWS), ROWS)], kv_r.at[0, 1]),
        pltpu.make_async_copy(q_ref.at[:, wide(h)], qb.at[h], q_r.at[0, 0]),
        pltpu.make_async_copy(go_ref.at[:, wide(h)], gb.at[h], q_r.at[0, 1]),
    ]
    for copy in own:
        copy.start()

    barrier = pltpu.get_barrier_semaphore()
    for i in range(1, PEERS):
        pl.semaphore_signal(barrier, inc=1, device_id=(c, to(i)), device_id_type=MESH)
    pl.semaphore_signal(barrier, inc=1, device_id=(after, h), device_id_type=MESH)
    pl.semaphore_signal(barrier, inc=1, device_id=(before, h), device_id_type=MESH)
    pl.semaphore_wait(barrier, PEERS + 1)

    def remote(src, dst, send, recv, device):
        return pltpu.make_async_remote_copy(
            src_ref=src, dst_ref=dst, send_sem=send, recv_sem=recv,
            device_id=device, device_id_type=MESH,
        )

    sends = []
    mine = pl.ds(pl.multiple_of(3 * SHARD + h * ROWS, ROWS), ROWS)
    for i in range(1, PEERS):
        p = to(i)
        for n, (src, dst) in enumerate(((k_ref, kw), (v_ref, vw))):
            copy = remote(src.at[:, narrow(p)], dst.at[mine], kv_s.at[i, n], kv_r.at[i, n], (c, p))
            copy.start()
            sends.append(copy)
    for i in range(1, PEERS):
        p = to(i)
        for n, (src, dst) in enumerate(((q_ref, qb), (go_ref, gb))):
            copy = remote(src.at[:, wide(p)], dst.at[h], q_s.at[i, n], q_r.at[i, n], (c, p))
            copy.start()
            sends.append(copy)

    for i in range(PEERS):
        for n, dst in enumerate((kw, vw)):
            piece = dst.at[pl.ds(pl.multiple_of(3 * SHARD + source(i) * ROWS, ROWS), ROWS)]
            pltpu.make_async_copy(piece, piece, kv_r.at[i, n]).wait()

    def ring(step):
        out = []
        for half in range(2):
            for n, buf in enumerate((kw, vw)):
                src = buf.at[pl.ds((3 - step) * SHARD + half * 128, 128)]
                dst = buf.at[pl.ds((2 - step) * SHARD + half * 128, 128)]
                at = half * 2 + n
                out.append(remote(src, dst, z_s.at[step, at], z_r.at[step, at], (after, h)))
        return out

    def transposed(block):
        at = pl.ds(block * SHARD, SHARD)
        kt[:, at] = kw[at, :].T
        vt[:, at] = vw[at, :].T

    steps = [ring(step) for step in range(REACH)]
    for copy in steps[0]:
        copy.start()

    eye = lax.broadcasted_iota(jnp.int32, (128, 128), 0) == lax.broadcasted_iota(jnp.int32, (128, 128), 1)
    doc_rows = []
    for tile in range(8):
        row = 2 * c - 6 + tile
        line = doc_ref[pl.ds(jnp.maximum(row, 0), 1), :].astype(F32)
        line = jnp.where(row >= 0, line, -1.0)
        doc_rows.append(line)
        column = jnp.sum(jnp.where(eye, jnp.broadcast_to(line, (128, 128)), 0.0), axis=1, keepdims=True)
        kd[tile * 128 : (tile + 1) * 128, :] = jnp.broadcast_to(column, (128, 128))
    lane = lax.broadcasted_iota(jnp.int32, (1, 128), 1)
    key_row = lax.broadcasted_iota(jnp.int32, (128, 128), 0)
    for r in range(PEERS):
        start = 128 * (r // 4)
        line = jnp.where(lane // ROWS == r % 4, doc_rows[6 + r // 4], 0.0)
        line = line + pltpu.roll(line, 32, 1) + pltpu.roll(line, 64, 1) + pltpu.roll(line, 96, 1)
        position = REACH * SHARD + r * ROWS + lane % ROWS
        for tile in range(7):
            at = start + tile * 128
            seen = kd[at : at + 128, :] == line
            if at + 128 > REACH * SHARD:
                seen = seen & (key_row + at <= position)
            bias[r, tile * 128 : (tile + 1) * 128, :] = jnp.where(seen, 0.0, -1e30)

    transposed(3)
    for step in range(REACH):
        for at, copy in enumerate(steps[step]):
            copy.wait_recv()
            if step < REACH - 1:
                steps[step + 1][at].start()
        transposed(2 - step)

    def forward(i, carry):
        r = source(i)
        for n, buf in enumerate((qb, gb)):
            pltpu.make_async_copy(buf.at[r], buf.at[r], q_r.at[i, n]).wait()
        start = pl.multiple_of(128 * (r // 4), 128)
        keys = pl.ds(start, SPAN)
        lanes = pl.ds(pl.multiple_of(r * 256, 256), 256)
        q2 = jnp.concatenate([qb[r, :, j * HD : (j + 1) * HD] for j in range(8)], axis=0)
        g2 = jnp.concatenate([gb[r, :, j * HD : (j + 1) * HD] for j in range(8)], axis=0)
        qall[lanes, :] = q2
        scr[...] = dot(kw[keys, :], q2, NT)
        peak = jnp.full((8, 256), -3e38, F32)
        for tile in range(7):
            at = slice(tile * 128, (tile + 1) * 128)
            extra = bias[r, at, :]
            x = scr[at, :] * (SCALE * LOG2E) + jnp.concatenate([extra, extra], axis=1)
            scr[at, :] = x
            peak = jnp.maximum(peak, jnp.max(x.reshape(16, 8, 256), axis=0))
        peak = jnp.max(peak, axis=0, keepdims=True)
        total = jnp.zeros((8, 256), F32)
        for tile in range(7):
            e = jnp.exp2(scr[tile * 128 : (tile + 1) * 128, :] - peak)
            total = total + jnp.sum(e.reshape(16, 8, 256), axis=0)
            eall[pl.ds(start + tile * 128, 128), lanes] = e.astype(BF16)
        inverse = 1.0 / jnp.sum(total, axis=0, keepdims=True)
        o_t = dot(vt[:, keys], eall[keys, lanes]) * inverse
        o2 = o_t.T.astype(BF16)
        for j in range(8):
            ob[r, :, j * HD : (j + 1) * HD] = o2[j * ROWS : (j + 1) * ROWS, :]
        g_t = g2.astype(F32).T
        delta = jnp.sum(g_t * o_t.astype(BF16).astype(F32), axis=0, keepdims=True) * inverse
        scaled = (g_t * inverse).astype(BF16)
        got[:, lanes] = scaled
        scr[...] = dot(vw[keys, :], scaled)
        for tile in range(7):
            rows = pl.ds(start + tile * 128, 128)
            ds = eall[rows, lanes].astype(F32) * (scr[tile * 128 : (tile + 1) * 128, :] - delta)
            dsall[rows, lanes] = ds.astype(BF16)

        @pl.when(i > 0)
        def _():
            remote(ob.at[r], att_ref.at[:, wide(h)], o_s.at[i], o_r.at[i], (c, r)).start()

        @pl.when(i == 0)
        def _():
            pltpu.make_async_copy(ob.at[r], att_ref.at[:, wide(h)], o_r.at[0]).start()

        return carry

    lax.fori_loop(0, PEERS, forward, 0)

    def gradients(block):
        for sub in range(2):
            tile = 2 * block + sub
            rows = slice(tile * 128, (tile + 1) * 128)
            lo, hi = (0, 1024) if tile == 0 else (1024, 2048) if tile == 7 else (0, 2048)
            part[0, rows, :] = dot(dsall[rows, lo:hi], qall[lo:hi, :]) * SCALE
            part[1, rows, :] = dot(eall[rows, lo:hi], got[:, lo:hi], NT)

    def relay(step):
        return [
            remote(sendk.at[step, n], recvk.at[step, n], w_s.at[step, n], w_r.at[step, n], (before, h))
            for n in range(2)
        ]

    relays = [relay(step) for step in range(REACH)]
    gradients(0)
    for n in range(2):
        sendk[0, n] = part[n, 0:SHARD, :].astype(BF16)
        relays[0][n].start()
    for block in range(1, REACH + 1):
        gradients(block)

    def query_gradients(i, carry):
        r = source(i)
        keys = pl.ds(pl.multiple_of(128 * (r // 4), 128), SPAN)
        lanes = pl.ds(pl.multiple_of(r * 256, 256), 256)
        dq = (dot(kt[:, keys], dsall[keys, lanes]) * SCALE).T.astype(BF16)
        for j in range(8):
            gqb[r, :, j * HD : (j + 1) * HD] = dq[j * ROWS : (j + 1) * ROWS, :]

        @pl.when(i > 0)
        def _():
            remote(gqb.at[r], gq_ref.at[:, wide(h)], g_s.at[i], g_r.at[i], (c, r)).start()

        @pl.when(i == 0)
        def _():
            pltpu.make_async_copy(gqb.at[r], gq_ref.at[:, wide(h)], g_r.at[0]).start()

        return carry

    lax.fori_loop(0, PEERS, query_gradients, 0)
    for step in range(REACH):
        block = slice((step + 1) * SHARD, (step + 2) * SHARD)
        for n in range(2):
            relays[step][n].wait_recv()
            total = recvk[step, n].astype(F32) + part[n, block, :]
            if step < REACH - 1:
                sendk[step + 1, n] = total.astype(BF16)
                relays[step + 1][n].start()
            else:
                fin[n] = total.astype(BF16)
    last = []
    for n, out in enumerate((gk_ref, gv_ref)):
        copy = pltpu.make_async_copy(fin.at[n, rows_of(h)], out.at[:, narrow(h)], f_r.at[0, n])
        copy.start()
        for i in range(1, PEERS):
            p = to(i)
            copy = remote(fin.at[n, rows_of(p)], out.at[:, narrow(h)], f_s.at[i, n], f_r.at[i, n], (c, p))
            copy.start()
            last.append(copy)

    for copy in sends + last:
        copy.wait_send()
    for step in range(REACH):
        for copy in steps[step] + relays[step]:
            copy.wait_send()
    for i in range(1, PEERS):
        r = source(i)
        remote(ob.at[r], att_ref.at[:, wide(h)], o_s.at[i], o_r.at[i], (c, r)).wait_send()
        remote(gqb.at[r], gq_ref.at[:, wide(h)], g_s.at[i], g_r.at[i], (c, r)).wait_send()
    for i in range(PEERS):
        p = to(i)
        for ref, sem in ((att_ref, o_r), (gq_ref, g_r)):
            piece = ref.at[:, wide(p)]
            pltpu.make_async_copy(piece, piece, sem.at[i]).wait()
        for n, ref in enumerate((gk_ref, gv_ref)):
            piece = ref.at[:, narrow(source(i))]
            pltpu.make_async_copy(piece, piece, f_r.at[i, n]).wait()


def body(queries, keys, values, documents, grad_out):
    any_spec = pl.BlockSpec(memory_space=pl.ANY)
    dma = pltpu.SemaphoreType.DMA
    return pl.pallas_call(
        kernel,
        out_shape=(
            jax.ShapeDtypeStruct((ROWS, PEERS * GW), BF16),
            jax.ShapeDtypeStruct((ROWS, PEERS * GW), BF16),
            jax.ShapeDtypeStruct((ROWS, PEERS * HD), BF16),
            jax.ShapeDtypeStruct((ROWS, PEERS * HD), BF16),
        ),
        in_specs=[any_spec, any_spec, any_spec, pl.BlockSpec(memory_space=pltpu.VMEM), any_spec],
        out_specs=(any_spec,) * 4,
        scratch_shapes=[
            pltpu.VMEM((PEERS, ROWS, GW), BF16),
            pltpu.VMEM((PEERS, ROWS, GW), BF16),
            pltpu.VMEM((WIN, HD), BF16),
            pltpu.VMEM((WIN, HD), BF16),
            pltpu.VMEM((HD, WIN), BF16),
            pltpu.VMEM((HD, WIN), BF16),
            pltpu.VMEM((2048, HD), BF16),
            pltpu.VMEM((HD, 2048), BF16),
            pltpu.VMEM((WIN, 128), F32),
            pltpu.VMEM((PEERS, SPAN, 128), F32),
            pltpu.VMEM((SPAN, 256), F32),
            pltpu.VMEM((WIN, 2048), BF16),
            pltpu.VMEM((WIN, 2048), BF16),
            pltpu.VMEM((PEERS, ROWS, GW), BF16),
            pltpu.VMEM((PEERS, ROWS, GW), BF16),
            pltpu.VMEM((2, WIN, HD), F32),
            pltpu.VMEM((REACH, 2, SHARD, HD), BF16),
            pltpu.VMEM((REACH, 2, SHARD, HD), BF16),
            pltpu.VMEM((2, SHARD, HD), BF16),
            dma((PEERS, 2)), dma((PEERS, 2)),
            dma((PEERS, 2)), dma((PEERS, 2)),
            dma((REACH, 4)), dma((REACH, 4)),
            dma((PEERS,)), dma((PEERS,)),
            dma((PEERS,)), dma((PEERS,)),
            dma((REACH, 2)), dma((REACH, 2)),
            dma((PEERS, 2)), dma((PEERS, 2)),
        ],
        compiler_params=pltpu.CompilerParams(
            collective_id=0, has_side_effects=True, vmem_limit_bytes=48 * 1024 * 1024
        ),
    )(queries, keys, values, documents.reshape(128, 128), grad_out)


def solution(mesh):
    split = P(("ctx", "kvh"), None)
    return jax.shard_map(
        body,
        mesh=mesh,
        in_specs=(split, split, split, P(), split),
        out_specs=(split,) * 4,
        check_vma=False,
    )
```

time: 168 us -> 67.2 us (0.40)
  the two profiles are of different devices: /device:TPU:7 before, /device:TPU:1 now
where the time goes in v1:
time: 67.2 us; the launch traced here: 66.9 us
  Pallas kernels  58.8 us (88%)
  local copies, waits for them, and re-layouts  7.44 us (11%)
    pallas_call x1, Pallas kernels, body(): pl.pallas_call(kernel, out_shape=(jax.ShapeDtypeStruct((ROWS, PEERS * GW)...  58.8 us
    unnamed x14, local copies, waits for them, and re-layouts  7.44 us

profile of v1, /device:TPU:1, one launch (start us, length us, event | category | flops | bytes accessed | tf_op | source)
XLA Modules:
  0.0 66.9 jit_solution(12199366336561761963)
XLA Ops:
  0.6 0.0 copy-start
  0.6 1.0 %copy-done = bf16[32,8192]{1,0:T(8,128)(2,1)S(1)} copy-done((bf16[32,8192]{1,0:T(8,128)(2,1)S(1)}, bf16[32,8192]{1,0:T(8,128)(2,1)}, u32[]{:S(2)}) %copy-start) | copy-done | bytes 524312
  1.7 0.0 copy-start.1
  1.7 1.0 %copy-done.1 = bf16[32,8192]{1,0:T(8,128)(2,1)S(1)} copy-done((bf16[32,8192]{1,0:T(8,128)(2,1)S(1)}, bf16[32,8192]{1,0:T(8,128)(2,1)}, u32[]{:S(2)}) %copy-start.1) | copy-done | bytes 524312
  2.7 0.0 copy-start.2
  2.7 0.8 %copy-done.2 = bf16[32,1024]{1,0:T(8,128)(2,1)S(1)} copy-done((bf16[32,1024]{1,0:T(8,128)(2,1)S(1)}, bf16[32,1024]{1,0:T(8,128)(2,1)}, u32[]{:S(2)}) %copy-start.2) | copy-done | bytes 65560
  3.6 0.0 copy-start.3
  3.6 0.8 %copy-done.3 = bf16[32,1024]{1,0:T(8,128)(2,1)S(1)} copy-done((bf16[32,1024]{1,0:T(8,128)(2,1)S(1)}, bf16[32,1024]{1,0:T(8,128)(2,1)}, u32[]{:S(2)}) %copy-start.3) | copy-done | bytes 65560
  4.4 0.0 copy-start.4
  4.4 0.8 %copy-done.4 = s32[16384]{0:T(1024)S(1)} copy-done((s32[16384]{0:T(1024)S(1)}, s32[16384]{0:T(1024)}, u32[]{:S(2)}) %copy-start.4) | copy-done | bytes 65560
  5.2 58.8 %shard_map.84 = (bf16[32,8192]{1,0:T(8,128)(2,1)S(1)}, bf16[32,8192]{1,0:T(8,128)(2,1)S(1)}, bf16[32,1024]{1,0:T(8,128)(2,1)S(1)}, bf16[32,1024]{1,0:T(8,128)(2,1)S(1)}) custom-call(bf16[32,8192]{1,0:T(8,128)(2,1)S(1)} %copy-done, bf16[32,1024]{1,0:T(8,128)(2,1)S(1)} %copy-done.2, bf16[32,1024]{1,0:T(8,128)(2,1)S(1)} %copy-done.3, s32[128,128]{1,0:T(8,128)S(1)} %bitcast.1, ...), custom_call_target="tpu_custom_call" | custom-call | tf_op jit(solution)/shard_map/pallas_call | solution.py:287
  64.0 0.8 %copy.13 = bf16[32,8192]{1,0:T(8,128)(2,1)} copy(bf16[32,8192]{1,0:T(8,128)(2,1)S(1)} %get-tuple-element.8) | data formatting | bytes 1048576
  64.8 0.8 %copy.14 = bf16[32,8192]{1,0:T(8,128)(2,1)} copy(bf16[32,8192]{1,0:T(8,128)(2,1)S(1)} %get-tuple-element.9) | data formatting | bytes 1048576
  65.6 0.6 copy.15
  66.2 0.6 copy.16
Async XLA Ops:
  0.6 1.0 %copy-start = (bf16[32,8192]{1,0:T(8,128)(2,1)S(1)}, bf16[32,8192]{1,0:T(8,128)(2,1)}, u32[]{:S(2)}) copy-start(bf16[32,8192]{1,0:T(8,128)(2,1)} %q_ref.1) | copy-start | bytes 1572868
  1.7 1.0 %copy-start.1 = (bf16[32,8192]{1,0:T(8,128)(2,1)S(1)}, bf16[32,8192]{1,0:T(8,128)(2,1)}, u32[]{:S(2)}) copy-start(bf16[32,8192]{1,0:T(8,128)(2,1)} %go_ref.1) | copy-start | bytes 1572868
  2.7 0.8 %copy-start.2 = (bf16[32,1024]{1,0:T(8,128)(2,1)S(1)}, bf16[32,1024]{1,0:T(8,128)(2,1)}, u32[]{:S(2)}) copy-start(bf16[32,1024]{1,0:T(8,128)(2,1)} %k_ref.1) | copy-start | bytes 196612
  3.6 0.8 %copy-start.3 = (bf16[32,1024]{1,0:T(8,128)(2,1)S(1)}, bf16[32,1024]{1,0:T(8,128)(2,1)}, u32[]{:S(2)}) copy-start(bf16[32,1024]{1,0:T(8,128)(2,1)} %v_ref.1) | copy-start | bytes 196612
  4.4 0.8 %copy-start.4 = (s32[16384]{0:T(1024)S(1)}, s32[16384]{0:T(1024)}, u32[]{:S(2)}) copy-start(s32[16384]{0:T(1024)} %param.8) | copy-start | bytes 196612

commit v2 on v1

--- a/solution.py
+++ b/solution.py
@@ -13,7 +13,9 @@
 ROWS = 32
 SHARD = 256
 WIN = 1024
-SPAN = 896
+SPAN = 800
+TILE = 160
+PAIR = 2
 GW = 1024
 SCALE = 1.0 / math.sqrt(HD)
 LOG2E = 1.4426950408889634
@@ -31,10 +33,12 @@
 def kernel(
     q_ref, k_ref, v_ref, doc_ref, go_ref,
     att_ref, gq_ref, gk_ref, gv_ref,
-    qb, gb, kw, vw, kt, vt, qall, got, kd, bias, scr, eall, dsall, ob, gqb,
+    qb, gb, kw, vw, kt, vt, qall, got, kd, bias, ob, gqb,
     part, sendk, recvk, fin,
     q_s, q_r, kv_s, kv_r, z_s, z_r, o_s, o_r, g_s, g_r, w_s, w_r, f_s, f_r,
+    *work,
 ):
+    scr, eall, dsall = work[:PAIR], work[PAIR : PAIR + PEERS], work[PAIR + PEERS :]
     c = lax.axis_index("ctx")
     h = lax.axis_index("kvh")
     shards = lax.axis_size("ctx")
@@ -70,9 +74,16 @@
     barrier = pltpu.get_barrier_semaphore()
     for i in range(1, PEERS):
         pl.semaphore_signal(barrier, inc=1, device_id=(c, to(i)), device_id_type=MESH)
-    pl.semaphore_signal(barrier, inc=1, device_id=(after, h), device_id_type=MESH)
-    pl.semaphore_signal(barrier, inc=1, device_id=(before, h), device_id_type=MESH)
-    pl.semaphore_wait(barrier, PEERS + 1)
+
+    @pl.when(c < shards - 1)
+    def _():
+        pl.semaphore_signal(barrier, inc=1, device_id=(after, h), device_id_type=MESH)
+
+    @pl.when(c > 0)
+    def _():
+        pl.semaphore_signal(barrier, inc=1, device_id=(before, h), device_id_type=MESH)
+
+    pl.semaphore_wait(barrier, PEERS - 1 + jnp.minimum(c, 1) + jnp.minimum(shards - 1 - c, 1))
 
     def remote(src, dst, send, recv, device):
         return pltpu.make_async_remote_copy(
@@ -116,8 +127,20 @@
         vt[:, at] = vw[at, :].T
 
     steps = [ring(step) for step in range(REACH)]
-    for copy in steps[0]:
-        copy.start()
+
+    @pl.when(c < shards - 1)
+    def _():
+        for copy in steps[0]:
+            copy.start()
+
+    @pl.when(c == 0)
+    def _():
+        kw[0 : REACH * SHARD, :] = jnp.zeros((REACH * SHARD, HD), BF16)
+        vw[0 : REACH * SHARD, :] = jnp.zeros((REACH * SHARD, HD), BF16)
+
+    @pl.when(c == shards - 1)
+    def _():
+        recvk[...] = jnp.zeros(recvk.shape, BF16)
 
     eye = lax.broadcasted_iota(jnp.int32, (128, 128), 0) == lax.broadcasted_iota(jnp.int32, (128, 128), 1)
     doc_rows = []
@@ -129,127 +152,151 @@
         column = jnp.sum(jnp.where(eye, jnp.broadcast_to(line, (128, 128)), 0.0), axis=1, keepdims=True)
         kd[tile * 128 : (tile + 1) * 128, :] = jnp.broadcast_to(column, (128, 128))
     lane = lax.broadcasted_iota(jnp.int32, (1, 128), 1)
-    key_row = lax.broadcasted_iota(jnp.int32, (128, 128), 0)
+    key_row = lax.broadcasted_iota(jnp.int32, (TILE, 128), 0)
     for r in range(PEERS):
-        start = 128 * (r // 4)
+        start = ROWS * r
         line = jnp.where(lane // ROWS == r % 4, doc_rows[6 + r // 4], 0.0)
         line = line + pltpu.roll(line, 32, 1) + pltpu.roll(line, 64, 1) + pltpu.roll(line, 96, 1)
         position = REACH * SHARD + r * ROWS + lane % ROWS
-        for tile in range(7):
-            at = start + tile * 128
-            seen = kd[at : at + 128, :] == line
-            if at + 128 > REACH * SHARD:
-                seen = seen & (key_row + at <= position)
-            bias[r, tile * 128 : (tile + 1) * 128, :] = jnp.where(seen, 0.0, -1e30)
+        for at in range(0, SPAN, TILE):
+            seen = kd[start + at : start + at + TILE, :] == line
+            if start + at + TILE > REACH * SHARD:
+                seen = seen & (key_row + (start + at) <= position)
+            bias[r, at : at + TILE, :] = jnp.where(seen, 0.0, -1e30)
+    for buf in (*eall, *dsall):
+        buf[...] = jnp.zeros(buf.shape, BF16)
 
     transposed(3)
     for step in range(REACH):
         for at, copy in enumerate(steps[step]):
-            copy.wait_recv()
+
+            @pl.when(c > 0)
+            def _(copy=copy):
+                copy.wait_recv()
+
             if step < REACH - 1:
-                steps[step + 1][at].start()
+
+                @pl.when(c < shards - 1)
+                def _(copy=steps[step + 1][at]):
+                    copy.start()
+
         transposed(2 - step)
 
-    def forward(i, carry):
-        r = source(i)
-        for n, buf in enumerate((qb, gb)):
-            pltpu.make_async_copy(buf.at[r], buf.at[r], q_r.at[i, n]).wait()
-        start = pl.multiple_of(128 * (r // 4), 128)
-        keys = pl.ds(start, SPAN)
-        lanes = pl.ds(pl.multiple_of(r * 256, 256), 256)
-        q2 = jnp.concatenate([qb[r, :, j * HD : (j + 1) * HD] for j in range(8)], axis=0)
-        g2 = jnp.concatenate([gb[r, :, j * HD : (j + 1) * HD] for j in range(8)], axis=0)
-        qall[lanes, :] = q2
-        scr[...] = dot(kw[keys, :], q2, NT)
+    def pieces(buf, r):
+        return jnp.concatenate([buf[r, :, j * HD : (j + 1) * HD] for j in range(8)], axis=0)
+
+    def scores(i, slot):
+        r = source(i)
+        keys = pl.ds(pl.multiple_of(r * ROWS, ROWS), SPAN)
+        q2 = pieces(qb, r)
+        qall[i * 256 : (i + 1) * 256, :] = q2
+        scr[slot][...] = dot(kw[keys, :], q2, NT)
+
+    def softmax(i, slot):
+        r = source(i)
         peak = jnp.full((8, 256), -3e38, F32)
-        for tile in range(7):
-            at = slice(tile * 128, (tile + 1) * 128)
-            extra = bias[r, at, :]
-            x = scr[at, :] * (SCALE * LOG2E) + jnp.concatenate([extra, extra], axis=1)
-            scr[at, :] = x
-            peak = jnp.maximum(peak, jnp.max(x.reshape(16, 8, 256), axis=0))
+        for at in range(0, SPAN, TILE):
+            extra = bias[r, at : at + TILE, :]
+            x = scr[slot][at : at + TILE, :] * (SCALE * LOG2E) + jnp.concatenate([extra, extra], axis=1)
+            scr[slot][at : at + TILE, :] = x
+            peak = jnp.maximum(peak, jnp.max(x.reshape(TILE // 8, 8, 256), axis=0))
         peak = jnp.max(peak, axis=0, keepdims=True)
         total = jnp.zeros((8, 256), F32)
-        for tile in range(7):
-            e = jnp.exp2(scr[tile * 128 : (tile + 1) * 128, :] - peak)
-            total = total + jnp.sum(e.reshape(16, 8, 256), axis=0)
-            eall[pl.ds(start + tile * 128, 128), lanes] = e.astype(BF16)
-        inverse = 1.0 / jnp.sum(total, axis=0, keepdims=True)
-        o_t = dot(vt[:, keys], eall[keys, lanes]) * inverse
+        for at in range(0, SPAN, TILE):
+            e = jnp.exp2(scr[slot][at : at + TILE, :] - peak)
+            total = total + jnp.sum(e.reshape(TILE // 8, 8, 256), axis=0)
+            eall[i][pl.ds(pl.multiple_of(r * ROWS + at, ROWS), TILE), :] = e.astype(BF16)
+        return 1.0 / jnp.sum(total, axis=0, keepdims=True)
+
+    def attend(i, inverse):
+        r = source(i)
+        o_t = dot(vt[...], eall[i][...]) * inverse
         o2 = o_t.T.astype(BF16)
         for j in range(8):
-            ob[r, :, j * HD : (j + 1) * HD] = o2[j * ROWS : (j + 1) * ROWS, :]
-        g_t = g2.astype(F32).T
+            ob[i, :, j * HD : (j + 1) * HD] = o2[j * ROWS : (j + 1) * ROWS, :]
+        g_t = pieces(gb, r).astype(F32).T
         delta = jnp.sum(g_t * o_t.astype(BF16).astype(F32), axis=0, keepdims=True) * inverse
-        scaled = (g_t * inverse).astype(BF16)
-        got[:, lanes] = scaled
-        scr[...] = dot(vw[keys, :], scaled)
-        for tile in range(7):
-            rows = pl.ds(start + tile * 128, 128)
-            ds = eall[rows, lanes].astype(F32) * (scr[tile * 128 : (tile + 1) * 128, :] - delta)
-            dsall[rows, lanes] = ds.astype(BF16)
-
-        @pl.when(i > 0)
-        def _():
-            remote(ob.at[r], att_ref.at[:, wide(h)], o_s.at[i], o_r.at[i], (c, r)).start()
-
-        @pl.when(i == 0)
-        def _():
-            pltpu.make_async_copy(ob.at[r], att_ref.at[:, wide(h)], o_r.at[0]).start()
-
-        return carry
-
-    lax.fori_loop(0, PEERS, forward, 0)
-
-    def gradients(block):
-        for sub in range(2):
-            tile = 2 * block + sub
-            rows = slice(tile * 128, (tile + 1) * 128)
-            lo, hi = (0, 1024) if tile == 0 else (1024, 2048) if tile == 7 else (0, 2048)
-            part[0, rows, :] = dot(dsall[rows, lo:hi], qall[lo:hi, :]) * SCALE
-            part[1, rows, :] = dot(eall[rows, lo:hi], got[:, lo:hi], NT)
-
-    def relay(step):
-        return [
+        got[:, i * 256 : (i + 1) * 256] = (g_t * inverse).astype(BF16)
+        return delta
+
+    def cotangents(i, slot):
+        keys = pl.ds(pl.multiple_of(source(i) * ROWS, ROWS), SPAN)
+        scr[slot][...] = dot(vw[keys, :], got[:, i * 256 : (i + 1) * 256])
+
+    def score_gradients(i, slot, delta):
+        r = source(i)
+        for at in range(0, SPAN, TILE):
+            rows = pl.ds(pl.multiple_of(r * ROWS + at, ROWS), TILE)
+            ds = eall[i][rows, :].astype(F32) * (scr[slot][at : at + TILE, :] - delta)
+            dsall[i][rows, :] = ds.astype(BF16)
+
+    def query_gradients(i):
+        dq = (dot(kt[...], dsall[i][...]) * SCALE).T.astype(BF16)
+        for j in range(8):
+            gqb[i, :, j * HD : (j + 1) * HD] = dq[j * ROWS : (j + 1) * ROWS, :]
+
+    def give(buf, out, send, recv, i):
+        r = source(i)
+        if i == 0:
+            return pltpu.make_async_copy(buf.at[0], out.at[:, wide(h)], recv.at[0])
+        return remote(buf.at[i], out.at[:, wide(h)], send.at[i], recv.at[i], (c, r))
+
+    for first in range(0, PEERS, PAIR):
+        group = range(first, first + PAIR)
+        for i in group:
+            for n, buf in enumerate((qb, gb)):
+                piece = buf.at[source(i)]
+                pltpu.make_async_copy(piece, piece, q_r.at[i, n]).wait()
+        for i in group:
+            scores(i, i % PAIR)
+        inverses = [softmax(i, i % PAIR) for i in group]
+        deltas = [attend(i, inverse) for i, inverse in zip(group, inverses)]
+        for i in group:
+            cotangents(i, i % PAIR)
+        for i, delta in zip(group, deltas):
+            score_gradients(i, i % PAIR, delta)
+        for i in group:
+            query_gradients(i)
+        for i in group:
+            give(ob, att_ref, o_s, o_r, i).start()
+            give(gqb, gq_ref, g_s, g_r, i).start()
+
+    def gradients(rows):
+        at = slice(rows[0], rows[1])
+        part[0, at, :] = dot(jnp.concatenate([buf[at, :] for buf in dsall], axis=1), qall[...]) * SCALE
+        part[1, at, :] = dot(jnp.concatenate([buf[at, :] for buf in eall], axis=1), got[...], NT)
+
+    relays = [
+        [
             remote(sendk.at[step, n], recvk.at[step, n], w_s.at[step, n], w_r.at[step, n], (before, h))
             for n in range(2)
         ]
-
-    relays = [relay(step) for step in range(REACH)]
-    gradients(0)
+        for step in range(REACH)
+    ]
+    gradients((0, SHARD))
     for n in range(2):
         sendk[0, n] = part[n, 0:SHARD, :].astype(BF16)
-        relays[0][n].start()
-    for block in range(1, REACH + 1):
-        gradients(block)
-
-    def query_gradients(i, carry):
-        r = source(i)
-        keys = pl.ds(pl.multiple_of(128 * (r // 4), 128), SPAN)
-        lanes = pl.ds(pl.multiple_of(r * 256, 256), 256)
-        dq = (dot(kt[:, keys], dsall[keys, lanes]) * SCALE).T.astype(BF16)
-        for j in range(8):
-            gqb[r, :, j * HD : (j + 1) * HD] = dq[j * ROWS : (j + 1) * ROWS, :]
-
-        @pl.when(i > 0)
-        def _():
-            remote(gqb.at[r], gq_ref.at[:, wide(h)], g_s.at[i], g_r.at[i], (c, r)).start()
-
-        @pl.when(i == 0)
-        def _():
-            pltpu.make_async_copy(gqb.at[r], gq_ref.at[:, wide(h)], g_r.at[0]).start()
-
-        return carry
-
-    lax.fori_loop(0, PEERS, query_gradients, 0)
+
+        @pl.when(c > 0)
+        def _(copy=relays[0][n]):
+            copy.start()
+
+    gradients((SHARD, WIN))
     for step in range(REACH):
         block = slice((step + 1) * SHARD, (step + 2) * SHARD)
         for n in range(2):
-            relays[step][n].wait_recv()
+
+            @pl.when(c < shards - 1)
+            def _(copy=relays[step][n]):
+                copy.wait_recv()
+
             total = recvk[step, n].astype(F32) + part[n, block, :]
             if step < REACH - 1:
                 sendk[step + 1, n] = total.astype(BF16)
-                relays[step + 1][n].start()
+
+                @pl.when(c > 0)
+                def _(copy=relays[step + 1][n]):
+                    copy.start()
             else:
                 fin[n] = total.astype(BF16)
     last = []
@@ -264,13 +311,22 @@
 
     for copy in sends + last:
         copy.wait_send()
-    for step in range(REACH):
-        for copy in steps[step] + relays[step]:
-            copy.wait_send()
+
+    @pl.when(c < shards - 1)
+    def _():
+        for step in range(REACH):
+            for copy in steps[step]:
+                copy.wait_send()
+
+    @pl.when(c > 0)
+    def _():
+        for step in range(REACH):
+            for copy in relays[step]:
+                copy.wait_send()
+
     for i in range(1, PEERS):
-        r = source(i)
-        remote(ob.at[r], att_ref.at[:, wide(h)], o_s.at[i], o_r.at[i], (c, r)).wait_send()
-        remote(gqb.at[r], gq_ref.at[:, wide(h)], g_s.at[i], g_r.at[i], (c, r)).wait_send()
+        give(ob, att_ref, o_s, o_r, i).wait_send()
+        give(gqb, gq_ref, g_s, g_r, i).wait_send()
     for i in range(PEERS):
         p = to(i)
         for ref, sem in ((att_ref, o_r), (gq_ref, g_r)):
@@ -305,9 +361,6 @@
             pltpu.VMEM((HD, 2048), BF16),
             pltpu.VMEM((WIN, 128), F32),
             pltpu.VMEM((PEERS, SPAN, 128), F32),
-            pltpu.VMEM((SPAN, 256), F32),
-            pltpu.VMEM((WIN, 2048), BF16),
-            pltpu.VMEM((WIN, 2048), BF16),
             pltpu.VMEM((PEERS, ROWS, GW), BF16),
             pltpu.VMEM((PEERS, ROWS, GW), BF16),
             pltpu.VMEM((2, WIN, HD), F32),
@@ -321,9 +374,11 @@
             dma((PEERS,)), dma((PEERS,)),
             dma((REACH, 2)), dma((REACH, 2)),
             dma((PEERS, 2)), dma((PEERS, 2)),
+            *[pltpu.VMEM((SPAN, 256), F32)] * PAIR,
+            *[pltpu.VMEM((WIN, 256), BF16)] * (2 * PEERS),
         ],
         compiler_params=pltpu.CompilerParams(
-            collective_id=0, has_side_effects=True, vmem_limit_bytes=48 * 1024 * 1024
+            collective_id=0, has_side_effects=True, vmem_limit_bytes=67043328
         ),
     )(queries, keys, values, documents.reshape(128, 128), grad_out)
 

time: 67.2 us -> 58.7 us (0.87)
  the two profiles are of different devices: /device:TPU:1 before, /device:TPU:7 now
where the time goes in v2:
time: 58.7 us; the launch traced here: 58.4 us
  Pallas kernels  53.4 us (91%)
  local copies, waits for them, and re-layouts  4.28 us (7%)
  between operations  0.65 us (1%)
    pallas_call x1, Pallas kernels, body(): pl.pallas_call(kernel, out_shape=(jax.ShapeDtypeStruct((ROWS, PEERS * GW)...  53.4 us
    unnamed x10, local copies, waits for them, and re-layouts  4.28 us

profile of v2, /device:TPU:7, one launch (start us, length us, event | category | flops | bytes accessed | tf_op | source)
XLA Modules:
  0.0 58.4 jit_solution(5449146400917365564)
XLA Ops:
  0.6 53.4 %shard_map.84 = (bf16[32,8192]{1,0:T(8,128)(2,1)}, bf16[32,8192]{1,0:T(8,128)(2,1)}, bf16[32,1024]{1,0:T(8,128)(2,1)}, bf16[32,1024]{1,0:T(8,128)(2,1)}) custom-call(bf16[32,8192]{1,0:T(8,128)(2,1)} %q_ref.1, bf16[32,1024]{1,0:T(8,128)(2,1)} %k_ref.1, bf16[32,1024]{1,0:T(8,128)(2,1)} %v_ref.1, s32[128,128]{1,0:T(8,128)} %bitcast.1, bf16[32,8192]{1,0:T(8,128)(2,1)} %go_ref.1), custom_call_target="tpu_custom_call" | custom-call | tf_op jit(solution)/shard_map/pallas_call | solution.py:343
  54.1 0.0 copy-start
  54.1 1.9 %copy.13 = bf16[32,8192]{1,0:T(8,128)(2,1)} copy(bf16[32,8192]{1,0:T(8,128)(2,1)} %get-tuple-element.8) | data formatting | bytes 1048576
  56.0 0.0 copy-done
  56.0 0.0 copy-start.2
  56.0 0.8 %copy.14 = bf16[32,8192]{1,0:T(8,128)(2,1)} copy(bf16[32,8192]{1,0:T(8,128)(2,1)S(1)} %copy-done) | data formatting | bytes 1048576
  56.8 0.1 copy-done.2
  56.9 0.0 copy-start.1
  56.9 0.6 %copy.15 = bf16[32,1024]{1,0:T(8,128)(2,1)} copy(bf16[32,1024]{1,0:T(8,128)(2,1)S(1)} %copy-done.2) | data formatting | bytes 131072
  57.5 0.2 copy-done.1
  57.8 0.6 %copy.16 = bf16[32,1024]{1,0:T(8,128)(2,1)} copy(bf16[32,1024]{1,0:T(8,128)(2,1)S(1)} %copy-done.1) | data formatting | bytes 131072
Async XLA Ops:
  54.1 1.9 %copy-start = (bf16[32,8192]{1,0:T(8,128)(2,1)S(1)}, bf16[32,8192]{1,0:T(8,128)(2,1)}, u32[]{:S(2)}) copy-start(bf16[32,8192]{1,0:T(8,128)(2,1)} %get-tuple-element.9) | copy-start | bytes 1572868
  56.0 0.9 %copy-start.2 = (bf16[32,1024]{1,0:T(8,128)(2,1)S(1)}, bf16[32,1024]{1,0:T(8,128)(2,1)}, u32[]{:S(2)}) copy-start(bf16[32,1024]{1,0:T(8,128)(2,1)} %get-tuple-element.10) | copy-start | bytes 196612
  56.9 0.9 %copy-start.1 = (bf16[32,1024]{1,0:T(8,128)(2,1)S(1)}, bf16[32,1024]{1,0:T(8,128)(2,1)}, u32[]{:S(2)}) copy-start(bf16[32,1024]{1,0:T(8,128)(2,1)} %get-tuple-element.11) | copy-start | bytes 196612

commit v3 on v2

--- a/solution.py
+++ b/solution.py
@@ -13,8 +13,7 @@
 ROWS = 32
 SHARD = 256
 WIN = 1024
-SPAN = 800
-TILE = 160
+TILE = 128
 PAIR = 2
 GW = 1024
 SCALE = 1.0 / math.sqrt(HD)
@@ -33,12 +32,12 @@
 def kernel(
     q_ref, k_ref, v_ref, doc_ref, go_ref,
     att_ref, gq_ref, gk_ref, gv_ref,
-    qb, gb, kw, vw, kt, vt, qall, got, kd, bias, ob, gqb,
+    qb, gb, kw, vw, kt, vt, qall, gotf, gotn, kd, bias, ob, gqb, near, gts, stats,
     part, sendk, recvk, fin,
     q_s, q_r, kv_s, kv_r, z_s, z_r, o_s, o_r, g_s, g_r, w_s, w_r, f_s, f_r,
     *work,
 ):
-    scr, eall, dsall = work[:PAIR], work[PAIR : PAIR + PEERS], work[PAIR + PEERS :]
+    scr, eall, dsall = work[: 2 * PAIR], work[2 * PAIR : 2 * PAIR + PEERS], work[2 * PAIR + PEERS :]
     c = lax.axis_index("ctx")
     h = lax.axis_index("kvh")
     shards = lax.axis_size("ctx")
@@ -154,20 +153,16 @@
     lane = lax.broadcasted_iota(jnp.int32, (1, 128), 1)
     key_row = lax.broadcasted_iota(jnp.int32, (TILE, 128), 0)
     for r in range(PEERS):
-        start = ROWS * r
         line = jnp.where(lane // ROWS == r % 4, doc_rows[6 + r // 4], 0.0)
         line = line + pltpu.roll(line, 32, 1) + pltpu.roll(line, 64, 1) + pltpu.roll(line, 96, 1)
         position = REACH * SHARD + r * ROWS + lane % ROWS
-        for at in range(0, SPAN, TILE):
-            seen = kd[start + at : start + at + TILE, :] == line
-            if start + at + TILE > REACH * SHARD:
-                seen = seen & (key_row + (start + at) <= position)
+        for at in range(0, WIN, TILE):
+            seen = kd[at : at + TILE, :] == line
+            if at >= REACH * SHARD:
+                seen = seen & (key_row + at <= position)
             bias[r, at : at + TILE, :] = jnp.where(seen, 0.0, -1e30)
-    for buf in (*eall, *dsall):
-        buf[...] = jnp.zeros(buf.shape, BF16)
-
-    transposed(3)
-    for step in range(REACH):
+
+    def arrive(step):
         for at, copy in enumerate(steps[step]):
 
             @pl.when(c > 0)
@@ -182,53 +177,68 @@
 
         transposed(2 - step)
 
+    transposed(3)
+    arrive(0)
+    arrive(1)
+
     def pieces(buf, r):
         return jnp.concatenate([buf[r, :, j * HD : (j + 1) * HD] for j in range(8)], axis=0)
 
-    def scores(i, slot):
+    def softmax(i, slot, lo, hi):
         r = source(i)
-        keys = pl.ds(pl.multiple_of(r * ROWS, ROWS), SPAN)
-        q2 = pieces(qb, r)
-        qall[i * 256 : (i + 1) * 256, :] = q2
-        scr[slot][...] = dot(kw[keys, :], q2, NT)
-
-    def softmax(i, slot):
-        r = source(i)
+        scr[slot][lo:hi, :] = dot(kw[lo:hi, :], qall[i * 256 : (i + 1) * 256, :], NT)
         peak = jnp.full((8, 256), -3e38, F32)
-        for at in range(0, SPAN, TILE):
+        for at in range(lo, hi, TILE):
             extra = bias[r, at : at + TILE, :]
             x = scr[slot][at : at + TILE, :] * (SCALE * LOG2E) + jnp.concatenate([extra, extra], axis=1)
             scr[slot][at : at + TILE, :] = x
             peak = jnp.maximum(peak, jnp.max(x.reshape(TILE // 8, 8, 256), axis=0))
         peak = jnp.max(peak, axis=0, keepdims=True)
         total = jnp.zeros((8, 256), F32)
-        for at in range(0, SPAN, TILE):
+        for at in range(lo, hi, TILE):
             e = jnp.exp2(scr[slot][at : at + TILE, :] - peak)
             total = total + jnp.sum(e.reshape(TILE // 8, 8, 256), axis=0)
-            eall[i][pl.ds(pl.multiple_of(r * ROWS + at, ROWS), TILE), :] = e.astype(BF16)
-        return 1.0 / jnp.sum(total, axis=0, keepdims=True)
-
-    def attend(i, inverse):
+            eall[i][at : at + TILE, :] = e.astype(BF16)
+        return peak, jnp.sum(total, axis=0, keepdims=True), dot(vt[:, lo:hi], eall[i][lo:hi, :])
+
+    def ahead(i, slot):
         r = source(i)
-        o_t = dot(vt[...], eall[i][...]) * inverse
+        qall[i * 256 : (i + 1) * 256, :] = pieces(qb, r)
+        gts[i] = pieces(gb, r).astype(F32).T
+        peak, total, term = softmax(i, slot, SHARD, WIN)
+        near[i] = term
+        stats[i, 0:1, :] = peak
+        stats[i, 1:2, :] = total
+
+    def attend(i, slot):
+        far_peak, far_total, term = softmax(i, slot, 0, SHARD)
+        peak = jnp.maximum(far_peak, stats[i, 0:1, :])
+        far = jnp.exp2(far_peak - peak)
+        close = jnp.exp2(stats[i, 0:1, :] - peak)
+        inverse = 1.0 / (far_total * far + stats[i, 1:2, :] * close)
+        far = far * inverse
+        close = close * inverse
+        o_t = (term * far + near[i] * close).astype(BF16).astype(F32)
         o2 = o_t.T.astype(BF16)
         for j in range(8):
             ob[i, :, j * HD : (j + 1) * HD] = o2[j * ROWS : (j + 1) * ROWS, :]
-        g_t = pieces(gb, r).astype(F32).T
-        delta = jnp.sum(g_t * o_t.astype(BF16).astype(F32), axis=0, keepdims=True) * inverse
-        got[:, i * 256 : (i + 1) * 256] = (g_t * inverse).astype(BF16)
-        return delta
+        g_t = gts[i]
+        delta = jnp.sum(g_t * o_t, axis=0, keepdims=True)
+        gotf[:, i * 256 : (i + 1) * 256] = (g_t * far).astype(BF16)
+        gotn[:, i * 256 : (i + 1) * 256] = (g_t * close).astype(BF16)
+        return delta * far, delta * close
+
+    ranges = ((0, SHARD, gotf), (SHARD, WIN, gotn))
 
     def cotangents(i, slot):
-        keys = pl.ds(pl.multiple_of(source(i) * ROWS, ROWS), SPAN)
-        scr[slot][...] = dot(vw[keys, :], got[:, i * 256 : (i + 1) * 256])
-
-    def score_gradients(i, slot, delta):
-        r = source(i)
-        for at in range(0, SPAN, TILE):
-            rows = pl.ds(pl.multiple_of(r * ROWS + at, ROWS), TILE)
-            ds = eall[i][rows, :].astype(F32) * (scr[slot][at : at + TILE, :] - delta)
-            dsall[i][rows, :] = ds.astype(BF16)
+        for lo, hi, got in ranges:
+            scr[slot][lo:hi, :] = dot(vw[lo:hi, :], got[:, i * 256 : (i + 1) * 256])
+
+    def score_gradients(i, slot, deltas):
+        for (lo, hi, _), delta in zip(ranges, deltas):
+            for at in range(lo, hi, TILE):
+                rows = slice(at, at + TILE)
+                dsall[i][rows, :] = (eall[i][rows, :].astype(F32) * (scr[slot][rows, :] - delta)).astype(BF16)
 
     def query_gradients(i):
         dq = (dot(kt[...], dsall[i][...]) * SCALE).T.astype(BF16)
@@ -241,66 +251,110 @@
             return pltpu.make_async_copy(buf.at[0], out.at[:, wide(h)], recv.at[0])
         return remote(buf.at[i], out.at[:, wide(h)], send.at[i], recv.at[i], (c, r))
 
-    for first in range(0, PEERS, PAIR):
+    def begin(first):
         group = range(first, first + PAIR)
         for i in group:
             for n, buf in enumerate((qb, gb)):
                 piece = buf.at[source(i)]
                 pltpu.make_async_copy(piece, piece, q_r.at[i, n]).wait()
+
+    def early(first):
+        return [attend(i, i % PAIR) for i in range(first, first + PAIR)]
+
+    def late(first, deltas):
+        group = range(first, first + PAIR)
         for i in group:
-            scores(i, i % PAIR)
-        inverses = [softmax(i, i % PAIR) for i in group]
-        deltas = [attend(i, inverse) for i, inverse in zip(group, inverses)]
-        for i in group:
-            cotangents(i, i % PAIR)
+            cotangents(i, PAIR + i % PAIR)
         for i, delta in zip(group, deltas):
-            score_gradients(i, i % PAIR, delta)
+            score_gradients(i, PAIR + i % PAIR, delta)
         for i in group:
             query_gradients(i)
-        for i in group:
+
+    pairs = (0, 2, 6, 4)
+    split = 3
+
+    def prepare(place):
+        begin(pairs[place])
+        for i in range(pairs[place], pairs[place] + PAIR):
+            ahead(i, place % 2 * PAIR + i % PAIR)
+
+    for place in range(split):
+        prepare(place)
+    arrive(2)
+    deltas = early(pairs[0])
+    for place in range(1, len(pairs)):
+        before_it = pairs[place - 1]
+        for i in range(before_it, before_it + PAIR):
             give(ob, att_ref, o_s, o_r, i).start()
+        if place + split - 1 < len(pairs):
+            prepare(place + split - 1)
+        late(before_it, deltas)
+        deltas = early(pairs[place])
+        for i in range(before_it, before_it + PAIR):
             give(gqb, gq_ref, g_s, g_r, i).start()
-
-    def gradients(rows):
-        at = slice(rows[0], rows[1])
-        part[0, at, :] = dot(jnp.concatenate([buf[at, :] for buf in dsall], axis=1), qall[...]) * SCALE
-        part[1, at, :] = dot(jnp.concatenate([buf[at, :] for buf in eall], axis=1), got[...], NT)
-
+    final = pairs[-1]
+    for i in range(final, final + PAIR):
+        give(ob, att_ref, o_s, o_r, i).start()
+    late(final, deltas)
+
+    def gradients(n, lo, hi):
+        at = slice(lo, hi)
+        if n == 0:
+            part[0, at, :] = dot(jnp.concatenate([buf[at, :] for buf in dsall], axis=1), qall[...]) * SCALE
+        else:
+            got = gotf if hi == SHARD else gotn
+            part[1, at, :] = dot(jnp.concatenate([buf[at, :] for buf in eall], axis=1), got[...], NT)
+
+    halves = [(n, pl.ds(half * 128, 128), half * 2 + n) for half in range(2) for n in (1, 0)]
     relays = [
         [
-            remote(sendk.at[step, n], recvk.at[step, n], w_s.at[step, n], w_r.at[step, n], (before, h))
-            for n in range(2)
+            remote(sendk.at[step, n, at], recvk.at[step, n, at], w_s.at[step, place], w_r.at[step, place], (before, h))
+            for n, at, place in halves
         ]
         for step in range(REACH)
     ]
-    gradients((0, SHARD))
-    for n in range(2):
-        sendk[0, n] = part[n, 0:SHARD, :].astype(BF16)
+    gradients(1, 0, SHARD)
+    gradients(0, 0, SHARD)
+    for (n, at, place), copy in zip(halves, relays[0]):
+        sendk[0, n, at] = part[n, at, :].astype(BF16)
 
         @pl.when(c > 0)
-        def _(copy=relays[0][n]):
+        def _(copy=copy):
             copy.start()
 
-    gradients((SHARD, WIN))
+    for i in range(final, final + PAIR):
+        give(gqb, gq_ref, g_s, g_r, i).start()
+    gradients(1, SHARD, WIN)
+    gradients(0, SHARD, WIN)
+    for copy in sends:
+        copy.wait_send()
+
+    @pl.when(c < shards - 1)
+    def _():
+        for step in range(REACH):
+            for copy in steps[step]:
+                copy.wait_send()
+
+    last = []
     for step in range(REACH):
-        block = slice((step + 1) * SHARD, (step + 2) * SHARD)
-        for n in range(2):
+        for spot, (n, at, place) in enumerate(halves):
 
             @pl.when(c < shards - 1)
-            def _(copy=relays[step][n]):
+            def _(copy=relays[step][spot]):
                 copy.wait_recv()
 
-            total = recvk[step, n].astype(F32) + part[n, block, :]
+            mine = pl.ds((step + 1) * SHARD + at.start, 128)
+            total = (recvk[step, n, at].astype(F32) + part[n, mine, :]).astype(BF16)
             if step < REACH - 1:
-                sendk[step + 1, n] = total.astype(BF16)
+                sendk[step + 1, n, at] = total
 
                 @pl.when(c > 0)
-                def _(copy=relays[step + 1][n]):
+                def _(copy=relays[step + 1][spot]):
                     copy.start()
             else:
-                fin[n] = total.astype(BF16)
-    last = []
-    for n, out in enumerate((gk_ref, gv_ref)):
+                fin[n, at] = total
+    outs = (gk_ref, gv_ref)
+    for n, out in enumerate(outs):
         copy = pltpu.make_async_copy(fin.at[n, rows_of(h)], out.at[:, narrow(h)], f_r.at[0, n])
         copy.start()
         for i in range(1, PEERS):
@@ -309,15 +363,6 @@
             copy.start()
             last.append(copy)
 
-    for copy in sends + last:
-        copy.wait_send()
-
-    @pl.when(c < shards - 1)
-    def _():
-        for step in range(REACH):
-            for copy in steps[step]:
-                copy.wait_send()
-
     @pl.when(c > 0)
     def _():
         for step in range(REACH):
@@ -328,19 +373,34 @@
         give(ob, att_ref, o_s, o_r, i).wait_send()
         give(gqb, gq_ref, g_s, g_r, i).wait_send()
     for i in range(PEERS):
-        p = to(i)
         for ref, sem in ((att_ref, o_r), (gq_ref, g_r)):
-            piece = ref.at[:, wide(p)]
+            piece = ref.at[:, wide(to(i))]
             pltpu.make_async_copy(piece, piece, sem.at[i]).wait()
-        for n, ref in enumerate((gk_ref, gv_ref)):
+    for copy in last:
+        copy.wait_send()
+    for i in range(PEERS):
+        for n, ref in enumerate(outs):
             piece = ref.at[:, narrow(source(i))]
             pltpu.make_async_copy(piece, piece, f_r.at[i, n]).wait()
 
 
+def finish(*refs):
+    sources, outs, held, sem = refs[:4], refs[4:8], refs[8:12], refs[12]
+    into = [pltpu.make_async_copy(sources[n], held[n], sem.at[0, n]) for n in range(4)]
+    back = [pltpu.make_async_copy(held[n], outs[n], sem.at[1, n]) for n in range(4)]
+    for copy in into:
+        copy.start()
+    for arrived, copy in zip(into, back):
+        arrived.wait()
+        copy.start()
+    for copy in back:
+        copy.wait()
+
+
 def body(queries, keys, values, documents, grad_out):
-    any_spec = pl.BlockSpec(memory_space=pl.ANY)
+    held = pl.BlockSpec(memory_space=pltpu.HBM)
     dma = pltpu.SemaphoreType.DMA
-    return pl.pallas_call(
+    parts = pl.pallas_call(
         kernel,
         out_shape=(
             jax.ShapeDtypeStruct((ROWS, PEERS * GW), BF16),
@@ -348,8 +408,8 @@
             jax.ShapeDtypeStruct((ROWS, PEERS * HD), BF16),
             jax.ShapeDtypeStruct((ROWS, PEERS * HD), BF16),
         ),
-        in_specs=[any_spec, any_spec, any_spec, pl.BlockSpec(memory_space=pltpu.VMEM), any_spec],
-        out_specs=(any_spec,) * 4,
+        in_specs=[held, held, held, pl.BlockSpec(memory_space=pltpu.VMEM), held],
+        out_specs=(held,) * 4,
         scratch_shapes=[
             pltpu.VMEM((PEERS, ROWS, GW), BF16),
             pltpu.VMEM((PEERS, ROWS, GW), BF16),
@@ -359,10 +419,14 @@
             pltpu.VMEM((HD, WIN), BF16),
             pltpu.VMEM((2048, HD), BF16),
             pltpu.VMEM((HD, 2048), BF16),
+            pltpu.VMEM((HD, 2048), BF16),
             pltpu.VMEM((WIN, 128), F32),
-            pltpu.VMEM((PEERS, SPAN, 128), F32),
+            pltpu.VMEM((PEERS, WIN, 128), F32),
             pltpu.VMEM((PEERS, ROWS, GW), BF16),
             pltpu.VMEM((PEERS, ROWS, GW), BF16),
+            pltpu.VMEM((PEERS, HD, 256), F32),
+            pltpu.VMEM((PEERS, HD, 256), F32),
+            pltpu.VMEM((PEERS, 8, 256), F32),
             pltpu.VMEM((2, WIN, HD), F32),
             pltpu.VMEM((REACH, 2, SHARD, HD), BF16),
             pltpu.VMEM((REACH, 2, SHARD, HD), BF16),
@@ -372,15 +436,22 @@
             dma((REACH, 4)), dma((REACH, 4)),
             dma((PEERS,)), dma((PEERS,)),
             dma((PEERS,)), dma((PEERS,)),
-            dma((REACH, 2)), dma((REACH, 2)),
+            dma((REACH, 4)), dma((REACH, 4)),
             dma((PEERS, 2)), dma((PEERS, 2)),
-            *[pltpu.VMEM((SPAN, 256), F32)] * PAIR,
+            *[pltpu.VMEM((WIN, 256), F32)] * (2 * PAIR),
             *[pltpu.VMEM((WIN, 256), BF16)] * (2 * PEERS),
         ],
         compiler_params=pltpu.CompilerParams(
             collective_id=0, has_side_effects=True, vmem_limit_bytes=67043328
         ),
     )(queries, keys, values, documents.reshape(128, 128), grad_out)
+    return pl.pallas_call(
+        finish,
+        out_shape=[jax.ShapeDtypeStruct(part.shape, BF16) for part in parts],
+        in_specs=[held] * 4,
+        out_specs=[held] * 4,
+        scratch_shapes=[pltpu.VMEM(part.shape, BF16) for part in parts] + [dma((2, 4))],
+    )(*parts)
 
 
 def solution(mesh):

time: 58.7 us -> 56.1 us (0.956)
  local copies, waits for them, and re-layouts: 4.28 us -> 0 us
  Pallas kernels: 53.4 us -> 55.2 us
    unnamed x10 -> x0, local copies, waits for them, and re-layouts: 4.28 us -> none
    pallas_call x0 -> x1, Pallas kernels: none -> 2.11 us  [body(): pl.pallas_call(finish, out_shape=[jax.ShapeDtypeStruct(part.shape, BF16)...]
where the time goes in v3:
time: 56.1 us; the launch traced here: 55.8 us
  Pallas kernels  55.2 us (98%)
  between operations  0.64 us (1%)
    pallas_call x1, Pallas kernels, body(): pl.pallas_call(kernel, out_shape=(jax.ShapeDtypeStruct((ROWS, PEERS * GW)...  53.1 us
    pallas_call x1, Pallas kernels, body(): pl.pallas_call(finish, out_shape=[jax.ShapeDtypeStruct(part.shape, BF16)...  2.11 us

profile of v3, /device:TPU:7, one launch (start us, length us, event | category | flops | bytes accessed | tf_op | source)
XLA Modules:
  0.0 55.8 jit_solution(15238084069153125992)
XLA Ops:
  0.6 53.1 %shard_map.84 = (bf16[32,8192]{1,0:T(8,128)(2,1)}, bf16[32,8192]{1,0:T(8,128)(2,1)}, bf16[32,1024]{1,0:T(8,128)(2,1)}, bf16[32,1024]{1,0:T(8,128)(2,1)}) custom-call(bf16[32,8192]{1,0:T(8,128)(2,1)} %q_ref.1, bf16[32,1024]{1,0:T(8,128)(2,1)} %k_ref.1, bf16[32,1024]{1,0:T(8,128)(2,1)} %v_ref.1, s32[128,128]{1,0:T(8,128)} %bitcast.1, bf16[32,8192]{1,0:T(8,128)(2,1)} %go_ref.1), custom_call_target="tpu_custom_call" | custom-call | tf_op jit(solution)/shard_map/pallas_call | solution.py:403
  53.7 2.1 %shard_map.85 = (bf16[32,8192]{1,0:T(8,128)(2,1)}, bf16[32,8192]{1,0:T(8,128)(2,1)}, bf16[32,1024]{1,0:T(8,128)(2,1)}, bf16[32,1024]{1,0:T(8,128)(2,1)}) custom-call(bf16[32,8192]{1,0:T(8,128)(2,1)} %get-tuple-element.8.refs_0_, bf16[32,8192]{1,0:T(8,128)(2,1)} %get-tuple-element.9.refs_1_, bf16[32,1024]{1,0:T(8,128)(2,1)} %get-tuple-element.10.refs_2_, ...), custom_call_target="tpu_custom_call" | custom-call | tf_op jit(solution)/shard_map/pallas_call | solution.py:448

commit v4 on v3

--- a/solution.py
+++ b/solution.py
@@ -105,32 +105,33 @@
             copy.start()
             sends.append(copy)
 
+    def rows_in(block, i):
+        return pl.ds(pl.multiple_of(block * SHARD + source(i) * ROWS, ROWS), ROWS)
+
+    def ring(step):
+        out = []
+        for i in range(PEERS):
+            for n, buf in enumerate((kw, vw)):
+                src, dst = buf.at[rows_in(3 - step, i)], buf.at[rows_in(2 - step, i)]
+                at = i * 2 + n
+                out.append(remote(src, dst, z_s.at[step, at], z_r.at[step, at], (after, h)))
+        return out
+
+    steps = [ring(step) for step in range(REACH)]
     for i in range(PEERS):
         for n, dst in enumerate((kw, vw)):
-            piece = dst.at[pl.ds(pl.multiple_of(3 * SHARD + source(i) * ROWS, ROWS), ROWS)]
+            piece = dst.at[rows_in(3, i)]
             pltpu.make_async_copy(piece, piece, kv_r.at[i, n]).wait()
 
-    def ring(step):
-        out = []
-        for half in range(2):
-            for n, buf in enumerate((kw, vw)):
-                src = buf.at[pl.ds((3 - step) * SHARD + half * 128, 128)]
-                dst = buf.at[pl.ds((2 - step) * SHARD + half * 128, 128)]
-                at = half * 2 + n
-                out.append(remote(src, dst, z_s.at[step, at], z_r.at[step, at], (after, h)))
-        return out
+        @pl.when(c < shards - 1)
+        def _(copies=steps[0][2 * i : 2 * i + 2]):
+            for copy in copies:
+                copy.start()
 
     def transposed(block):
         at = pl.ds(block * SHARD, SHARD)
         kt[:, at] = kw[at, :].T
         vt[:, at] = vw[at, :].T
-
-    steps = [ring(step) for step in range(REACH)]
-
-    @pl.when(c < shards - 1)
-    def _():
-        for copy in steps[0]:
-            copy.start()
 
     @pl.when(c == 0)
     def _():
@@ -163,17 +164,19 @@
             bias[r, at : at + TILE, :] = jnp.where(seen, 0.0, -1e30)
 
     def arrive(step):
-        for at, copy in enumerate(steps[step]):
+        for i in range(PEERS):
 
             @pl.when(c > 0)
-            def _(copy=copy):
-                copy.wait_recv()
+            def _(copies=steps[step][2 * i : 2 * i + 2]):
+                for copy in copies:
+                    copy.wait_recv()
 
             if step < REACH - 1:
 
                 @pl.when(c < shards - 1)
-                def _(copy=steps[step + 1][at]):
-                    copy.start()
+                def _(copies=steps[step + 1][2 * i : 2 * i + 2]):
+                    for copy in copies:
+                        copy.start()
 
         transposed(2 - step)
 
@@ -433,7 +436,7 @@
             pltpu.VMEM((2, SHARD, HD), BF16),
             dma((PEERS, 2)), dma((PEERS, 2)),
             dma((PEERS, 2)), dma((PEERS, 2)),
-            dma((REACH, 4)), dma((REACH, 4)),
+            dma((REACH, 2 * PEERS)), dma((REACH, 2 * PEERS)),
             dma((PEERS,)), dma((PEERS,)),
             dma((PEERS,)), dma((PEERS,)),
             dma((REACH, 4)), dma((REACH, 4)),

time: 56.1 us -> 54.7 us (0.975)
  Pallas kernels: 55.2 us -> 53.8 us
    pallas_call x1, Pallas kernels: 53.1 us -> 51.7 us  [body(): pl.pallas_call(kernel, out_shape=(jax.ShapeDtypeStruct((ROWS, PEERS * GW)...]
where the time goes in v4:
time: 54.7 us; the launch traced here: 54.4 us
  Pallas kernels  53.8 us (98%)
  between operations  0.64 us (1%)
    pallas_call x1, Pallas kernels, body(): pl.pallas_call(kernel, out_shape=(jax.ShapeDtypeStruct((ROWS, PEERS * GW)...  51.7 us
    pallas_call x1, Pallas kernels, body(): pl.pallas_call(finish, out_shape=[jax.ShapeDtypeStruct(part.shape, BF16)...  2.11 us

profile of v4, /device:TPU:7, one launch (start us, length us, event | category | flops | bytes accessed | tf_op | source)
XLA Modules:
  0.0 54.4 jit_solution(5573350456555959390)
XLA Ops:
  0.6 51.7 %shard_map.84 = (bf16[32,8192]{1,0:T(8,128)(2,1)}, bf16[32,8192]{1,0:T(8,128)(2,1)}, bf16[32,1024]{1,0:T(8,128)(2,1)}, bf16[32,1024]{1,0:T(8,128)(2,1)}) custom-call(bf16[32,8192]{1,0:T(8,128)(2,1)} %q_ref.1, bf16[32,1024]{1,0:T(8,128)(2,1)} %k_ref.1, bf16[32,1024]{1,0:T(8,128)(2,1)} %v_ref.1, s32[128,128]{1,0:T(8,128)} %bitcast.1, bf16[32,8192]{1,0:T(8,128)(2,1)} %go_ref.1), custom_call_target="tpu_custom_call" | custom-call | tf_op jit(solution)/shard_map/pallas_call | solution.py:406
  52.3 2.1 %shard_map.85 = (bf16[32,8192]{1,0:T(8,128)(2,1)}, bf16[32,8192]{1,0:T(8,128)(2,1)}, bf16[32,1024]{1,0:T(8,128)(2,1)}, bf16[32,1024]{1,0:T(8,128)(2,1)}) custom-call(bf16[32,8192]{1,0:T(8,128)(2,1)} %get-tuple-element.8.refs_0_, bf16[32,8192]{1,0:T(8,128)(2,1)} %get-tuple-element.9.refs_1_, bf16[32,1024]{1,0:T(8,128)(2,1)} %get-tuple-element.10.refs_2_, ...), custom_call_target="tpu_custom_call" | custom-call | tf_op jit(solution)/shard_map/pallas_call | solution.py:451
